TPU v7x, 128 devices: a whole 4x4x4 slice. The times are simulated.
128 devices in a mesh: chan: 4 (over x_hi, core), half: 2 (over x_lo), ctx: 16 (over z, y).
Axes of the slice: x: 4 (x_hi: 2, x_lo: 2; x = x_hi * 2 + x_lo), y: 4, z: 4, core: 2. Of those that a mesh axis runs over, the one named last changes fastest.
Arguments:
- query_gate: bfloat16 [8192, 8192], P('ctx', 'chan'), parts along dimension 1, may hold values from -6 to 6
- key_gate: bfloat16 [8192, 8192], P('ctx', 'chan'), parts along dimension 1, may hold values from -6 to 6
- value_input: bfloat16 [8192, 8192], P('ctx', 'chan'), parts along dimension 1, may hold values from -6 to 6
- residues: float32 [16, 8192], P(None, 'chan'), parts along dimension 1, may hold values from -1.5 to 1.5
- decays: float32 [16, 8192], P(None, 'chan'), parts along dimension 1, may hold values from 6.1035157e-06 to 0.05
- skip_gain: float32 [8192], P('chan'), parts along dimension 0, may hold values from 0.25 to 1
Outputs:
- mixed: bfloat16 [8192, 8192], P('ctx', 'chan'), parts along dimension 1
There are 4 independent parts, one for each index of `chan`. A program takes and returns all parts, laid end to end along the dimension named above; each array names one. Nothing has to cross between parts.
All inputs are finite; a program needn't handle non-finite values.
Results may differ from a plain program's by a relative error of at most 0.00155.
Values may be sent and summed in bfloat16 or wider, within the bound.
A program may use at most 128 MiB of HBM per device.

v0:
```python
import math

import jax
import jax.numpy as jnp
from jax import lax
from jax.sharding import PartitionSpec as P


def unit_phase(phase_index, period, direction):
    phase_angle = phase_index.astype(jnp.float32) * (direction * 2.0 * math.pi / period)
    return (jnp.cos(phase_angle), jnp.sin(phase_angle))


def dft_table(length_n, direction):
    index_row = jnp.arange(length_n, dtype=jnp.int32)
    cosine, sine_part = unit_phase(
        index_row[:, None] * index_row[None, :] % length_n, length_n, direction
    )
    upper = jnp.concatenate([cosine, -sine_part], 1)
    lower = jnp.concatenate([sine_part, cosine], 1)
    return jnp.concatenate([upper, lower], 0)


def apply_table(field, matrix):
    lead_shape = field.shape
    flat_data = field.reshape(matrix.shape[0], -1)
    result = jnp.dot(
        matrix, flat_data, precision=lax.Precision.HIGHEST, preferred_element_type=jnp.float32
    )
    return result.reshape(lead_shape)


def rotate(field, cosine, sine_part):
    real_out = cosine * field[0] - sine_part * field[1]
    imag_out = sine_part * field[0] + cosine * field[1]
    return jnp.stack([real_out, imag_out])


def spectrum(frequency, residues, decays, half_bit, seq_len):
    row_count = frequency.shape[0]
    block_rows = math.gcd(row_count, 64)
    grouped = frequency.reshape(row_count // block_rows, block_rows)
    decay_mode = decays[:, None, :]
    damping = jnp.exp(-decay_mode)
    decay_gap = -jnp.expm1(-decay_mode)
    end_value = jnp.exp(-decay_mode * seq_len)
    numerator = jnp.where(half_bit == 0, -jnp.expm1(-decay_mode * seq_len), 1.0 + end_value)
    scaled = residues[:, None, :] * jnp.sqrt(decay_mode) * numerator

    def one_block(block_freq):
        theta_row = ((2 * block_freq + half_bit).astype(jnp.float32) * (math.pi / seq_len))[
            None, :, None
        ]
        half_sine = jnp.sin(0.5 * theta_row)
        real_den = decay_gap + 2.0 * damping * half_sine * half_sine
        imag_den = damping * jnp.sin(theta_row)
        factor = scaled / (real_den * real_den + imag_den * imag_den)
        return (jnp.sum(factor * real_den, 0), -jnp.sum(factor * imag_den, 0))

    real_part, imag_part = lax.map(one_block, grouped)
    return (real_part.reshape(row_count, -1), imag_part.reshape(row_count, -1))


def spread_positions(signal, residues, decays, half_bit, ctx_rank, ctx_size):
    row_count, chan_width = signal.shape
    seq_len = row_count * ctx_size
    group_rows = row_count // ctx_size
    positions = ctx_rank * row_count + jnp.arange(row_count, dtype=jnp.int32)
    cosine, sine_part = unit_phase(positions * half_bit % (2 * seq_len), 2 * seq_len, -1.0)
    field = jnp.stack([signal * cosine[:, None], signal * sine_part[:, None]]).reshape(
        2, ctx_size, group_rows, chan_width
    )
    field = lax.all_to_all(field, "ctx", split_axis=1, concat_axis=1, tiled=True)
    field = apply_table(field, dft_table(ctx_size, -1.0))
    inner_idx = ctx_rank * group_rows + jnp.arange(group_rows, dtype=jnp.int32)
    outer_idx = jnp.arange(ctx_size, dtype=jnp.int32)
    cosine, sine_part = unit_phase(outer_idx[:, None] * inner_idx[None, :] % seq_len, seq_len, -1.0)
    field = rotate(field, cosine[:, :, None], sine_part[:, :, None])
    field = lax.all_to_all(field, "ctx", split_axis=1, concat_axis=2, tiled=True).reshape(
        2, row_count, chan_width
    )
    field = apply_table(field, dft_table(row_count, -1.0))
    frequency = ctx_rank + ctx_size * jnp.arange(row_count, dtype=jnp.int32)
    real_h, imag_h = spectrum(frequency, residues, decays, half_bit, seq_len)
    field = rotate(field, real_h, imag_h)
    field = apply_table(field, dft_table(row_count, 1.0))
    cosine, sine_part = unit_phase(
        jnp.arange(row_count, dtype=jnp.int32) * ctx_rank % seq_len, seq_len, 1.0
    )
    field = rotate(field, cosine[:, None], sine_part[:, None]).reshape(
        2, ctx_size, group_rows, chan_width
    )
    field = lax.all_to_all(field, "ctx", split_axis=1, concat_axis=1, tiled=True)
    field = apply_table(field, dft_table(ctx_size, 1.0))
    position_map = outer_idx[:, None] * row_count + inner_idx[None, :]
    cosine, sine_part = unit_phase(position_map * half_bit % (2 * seq_len), 2 * seq_len, 1.0)
    half_term = (cosine[:, :, None] * field[0] - sine_part[:, :, None] * field[1]) * (0.5 / seq_len)
    return lax.all_to_all(half_term, "ctx", split_axis=0, concat_axis=1, tiled=True).reshape(
        row_count, chan_width
    )


def shards(query_gate, key_gate, value_input, residues, decays, skip_gain):
    ctx_size = lax.axis_size("ctx")
    ctx_rank = lax.axis_index("ctx")
    half_bit = lax.axis_index("half")
    signal = key_gate.astype(jnp.float32) * value_input.astype(jnp.float32)
    half_term = spread_positions(signal, residues, decays, half_bit, ctx_rank, ctx_size)
    full_conv = lax.psum(half_term, "half")
    return (query_gate.astype(jnp.float32) * (full_conv + skip_gain * signal)).astype(jnp.bfloat16)


def solution(mesh):
    placed = (
        P("ctx", "chan"),
        P("ctx", "chan"),
        P("ctx", "chan"),
        P(None, "chan"),
        P(None, "chan"),
        P("chan"),
    )
    return jax.shard_map(
        shards, mesh=mesh, in_specs=placed, out_specs=P("ctx", "chan"), check_vma=False
    )
```

profile of v0, /device:TPU:96, one launch (start us, length us, event | category | flops | bytes accessed | tf_op | source)
XLA Modules:
  0.0 711.2 jit_solution(4007284607748301417)
XLA Ops:
  13.4 7.3 %all-to-all-start = ((f32[2,16,32,2048]{3,2,0,1:T(8,128)}), f32[2,16,32,2048]{3,2,0,1:T(8,128)}, u32[]{:S(2)}, u32[]{:S(2)}) async-start(f32[2,16,32,2048]{3,2,0,1:T(8,128)} %pad_maximum_fusion), calls=%async_computation | async-start | bytes 16777216 | tf_op jit(solution)/shard_map/all_to_all | solution.py:73
  21.1 122.9 %all-to-all-done = f32[2,16,32,2048]{3,2,0,1:T(8,128)} async-done(((f32[2,16,32,2048]{3,2,0,1:T(8,128)}), f32[2,16,32,2048]{3,2,0,1:T(8,128)}, u32[]{:S(2)}, u32[]{:S(2)}) %all-to-all-start) | async-done | bytes 8388640 | tf_op jit(solution)/shard_map/all_to_all | solution.py:73
  144.1 4.0 copy.22
  148.0 4.9 copy.31
  152.9 8.3 %fusion.48 = f32[32,65536]{1,0:T(8,128)S(1)} fusion(f32[32,65536]{1,0:T(8,128)S(1)} %bitcast.129, f32[16,16]{1,0:T(8,128)S(1)} %get-tuple-element.155, f32[16,16]{1,0:T(8,128)S(1)} %get-tuple-element.154, f32[16,16]{1,0:T(8,128)S(1)} %fusion.75), kind=kOutput, calls=%fused_computation.84 | convolution fusion | flops 805309440 | bytes 16780288 | tf_op jit(solution)/shard_map/dot_general | solution.py:27
  172.5 6.7 all-to-all-start.1
  179.2 41.1 %while.14 = (s32[]{:T(128)}, f32[8,64,2048]{2,1,0:T(8,128)}, f32[8,64,2048]{2,1,0:T(8,128)}, f32[16,1,2048]{2,0,1:T(8,128)S(1)}, f32[16,1,2048]{2,0,1:T(8,128)S(...) while((s32[]{:T(128)}, f32[8,64,2048]{2,1,0:T(8,128)}, ...), condition=%wide.region_3.4_spmd, body=%wide.region_0.3_spmd.sunk | while | flops 25067904 | bytes 3934565 | solution.py:60
  179.3 4.0 fusion.98
  184.5 4.0 fusion.98
  189.6 4.0 fusion.98
  194.7 4.0 fusion.98
  199.9 4.0 fusion.98
  205.0 4.0 fusion.98
  210.1 4.0 fusion.98
  215.2 4.0 fusion.98
  220.4 4.6 fusion.39
  225.0 3.9 fusion.38
  228.9 5.0 multiply_sine_fusion
  233.8 5.3 multiply_sine_fusion.1
  239.1 61.3 %all-to-all-done.1 = f32[2,16,32,2048]{3,2,0,1:T(8,128)} async-done(((f32[2,16,32,2048]{3,2,0,1:T(8,128)}), f32[2,16,32,2048]{3,2,0,1:T(8,128)}, u32[]{:S(2)}, u32[]{:S(2)}) %all-to-all-start.1) | async-done | bytes 8388640 | tf_op jit(solution)/shard_map/all_to_all | solution.py:79
  300.4 4.1 copy.27
  304.7 29.5 %fusion.21 = f32[1024,2048]{1,0:T(8,128)} fusion(f32[1024,2048]{1,0:T(8,128)S(1)} %bitcast.148, f32[512,512]{1,0:T(8,128)S(1)} %copy-done.3, f32[512,512]{1,0:T(8,128)S(1)} %copy-done.2, f32[512,512]{1,0:T(8,128)S(1)} %copy-done.1), kind=kOutput, calls=%fused_computation.39 | convolution fusion | flops 25772949504 | bytes 19922944 | tf_op jit(solution)/shard_map/dot_general | solution.py:27
  334.1 10.2 %fusion.29 = (f32[512,2048]{1,0:T(8,128)S(1)}, f32[512,2048]{1,0:T(8,128)}) fusion(f32[8,64,2048]{2,1,0:T(8,128)} %get-tuple-element.108, f32[8,64,2048]{2,1,0:T(8,128)} %get-tuple-element.107, f32[1024,2048]{1,0:T(8,128)} %fusion.21), kind=kLoop, calls=%fused_computation.49 | loop fusion | flops 6291456 | bytes 25165824 | tf_op jit(solution)/shard_map/sub | solution.py:34
  347.1 30.9 %fusion.13 = f32[1024,2048]{1,0:T(8,128)S(1)} fusion(f32[1024,2048]{1,0:T(8,128)S(1)} %bitcast.147, f32[512,512]{1,0:T(8,128)} %get-tuple-element.159, f32[512,512]{1,0:T(8,128)S(1)} %get-tuple-element.158, f32[512,512]{1,0:T(8,128)S(1)} %fusion.38), kind=kOutput, calls=%fused_computation.31 | convolution fusion | flops 25772949504 | bytes 19922944 | tf_op jit(solution)/shard_map/dot_general | solution.py:27
  383.9 6.0 all-to-all-start.2
  390.3 118.8 %all-to-all-done.2 = f32[2,16,32,2048]{3,2,0,1:T(8,128)} async-done(((f32[2,16,32,2048]{3,2,0,1:T(8,128)}), f32[2,16,32,2048]{3,2,0,1:T(8,128)}, u32[]{:S(2)}, u32[]{:S(2)}) %all-to-all-start.2) | async-done | bytes 8388640 | tf_op jit(solution)/shard_map/all_to_all | solution.py:93
  509.1 4.0 copy.30
  513.1 4.9 copy.34
  518.0 8.4 %fusion.40 = f32[32,65536]{1,0:T(8,128)S(1)} fusion(f32[32,65536]{1,0:T(8,128)S(1)} %bitcast.130, f32[16,16]{1,0:T(8,128)S(1)} %get-tuple-element.161, f32[16,16]{1,0:T(8,128)S(1)} %get-tuple-element.160, f32[16,16]{1,0:T(8,128)S(1)} %fusion.74), kind=kOutput, calls=%fused_computation.76 | convolution fusion | flops 805309440 | bytes 16780288 | tf_op jit(solution)/shard_map/dot_general | solution.py:27
  532.5 51.0 %all_to_all.28 = f32[16,32,2048]{2,1,0:T(8,128)} all-to-all(f32[16,32,2048]{2,1,0:T(8,128)S(1)} %fusion.6), channel_id=1, replica_groups=mesh['chan'=4,'half'=2,'ctx'=16] {'ctx'}, dimensions={0} | all-to-all | bytes 8388608 | tf_op jit(solution)/shard_map/all_to_all | solution.py:98
  583.5 114.1 %all-reduce.2.cloned.1.call-done = f32[512,2048]{1,0:T(8,128)} async-done(((f32[512,2048]{1,0:T(8,128)}), f32[512,2048]{1,0:T(8,128)}) %all-reduce.2.cloned.1.call-update) | async-done | bytes 4194320 | tf_op jit(solution)/shard_map/psum | solution.py:109
  697.6 6.3 multiply_convert_fusion
  (75 shorter events, 43.1 us)
Async XLA Ops:
  13.4 7.6 %copy-start.4 = (f32[16,2048]{1,0:T(8,128)S(1)}, f32[16,2048]{1,0:T(8,128)}, u32[]{:S(2)}) copy-start(f32[16,2048]{1,0:T(8,128)} %param.12) | copy-start | bytes 393220
  13.4 7.6 %copy-start.5 = (f32[16,2048]{1,0:T(8,128)S(1)}, f32[16,2048]{1,0:T(8,128)}, u32[]{:S(2)}) copy-start(f32[16,2048]{1,0:T(8,128)} %param.11) | copy-start | bytes 393220
  13.4 130.7 %all-to-all-start = ((f32[2,16,32,2048]{3,2,0,1:T(8,128)}), f32[2,16,32,2048]{3,2,0,1:T(8,128)}, u32[]{:S(2)}, u32[]{:S(2)}) async-start(f32[2,16,32,2048]{3,2,0,1:T(8,128)} %pad_maximum_fusion), calls=%async_computation | async-start | bytes 16777216 | tf_op jit(solution)/shard_map/all_to_all | solution.py:73
  172.5 128.0 %all-to-all-start.1 = ((f32[2,16,32,2048]{3,2,0,1:T(8,128)}), f32[2,16,32,2048]{3,2,0,1:T(8,128)}, u32[]{:S(2)}, u32[]{:S(2)}) async-start(f32[2,16,32,2048]{3,2,0,1:T(8,128)} %pad_maximum_fusion.1), calls=%async_computation.1 | async-start | bytes 16777216 | tf_op jit(solution)/shard_map/all_to_all | solution.py:79
  300.4 4.1 copy-start.1
  300.4 4.1 copy-start.2
  300.4 4.2 copy-start.3
  383.9 125.2 %all-to-all-start.2 = ((f32[2,16,32,2048]{3,2,0,1:T(8,128)}), f32[2,16,32,2048]{3,2,0,1:T(8,128)}, u32[]{:S(2)}, u32[]{:S(2)}) async-start(f32[2,16,32,2048]{3,2,0,1:T(8,128)} %pad_maximum_fusion.3), calls=%async_computation.2 | async-start | bytes 16777216 | tf_op jit(solution)/shard_map/all_to_all | solution.py:93
  389.9 307.7 %all-reduce.2.cloned.1.call-start = ((), (), s32[]{:S(2)}) async-start(), calls=%async_computation.4 | async-start | bytes 8388608 | tf_op jit(solution)/shard_map/psum | solution.py:109
  583.5 114.1 %copy-start = (bf16[512,2048]{1,0:T(8,128)(2,1)S(1)}, bf16[512,2048]{1,0:T(8,128)(2,1)}, u32[]{:S(2)}) copy-start(bf16[512,2048]{1,0:T(8,128)(2,1)} %param.10) | copy-start | bytes 6291460
  583.5 114.1 %copy-start.6 = (f32[2048]{0:T(1024)S(1)}, f32[2048]{0:T(1024)}, u32[]{:S(2)}) copy-start(f32[2048]{0:T(1024)} %param.13) | copy-start | bytes 24580
Sparse Core Ops, SparseCore 0:
  583.7 113.9 all-reduce.1
where the time goes:
time: 723 us; the launch traced here: 711 us
  waiting for transfers between devices  417 us (58%)
  other arithmetic  98.7 us (14%)
  matrix products  77 us (11%)
  blocking collectives  51 us (7%)
  local copies, waits for them, and re-layouts  32.7 us (5%)
  starting transfers between devices  20.3 us (3%)
  between operations  14.1 us (2%)
    all_to_all x2, waiting for transfers between devices, spread_positions(): lax.all_to_all(field, 'ctx', split_axis=1, concat_axis=1, tiled=True)  242 us
    psum x1, waiting for transfers between devices, shards(): full_conv = lax.psum(half_term, 'half')  114 us
    dot_general x4, matrix products, apply_table(): jnp.dot(matrix, flat_data, precision=lax.Precision.HIGHEST, preferred_ele...  77 us
    all_to_all x1, waiting for transfers between devices, spread_positions(): lax.all_to_all(field, 'ctx', split_axis=1, concat_axis=2, tiled=True)  61.3 us
    all_to_all x1, blocking collectives, spread_positions(): lax.all_to_all(half_term, 'ctx', split_axis=0, concat_axis=1, tiled=True)  51 us
    reduce_sum x8, other arithmetic, one_block(): return (jnp.sum(factor * real_den, 0), -jnp.sum(factor * imag_den, 0))  31.6 us
    unnamed x20, local copies, waits for them, and re-layouts  19.6 us
  transfers between devices with their start and end apart: 4, of which 4 were waited for; matrix products, arithmetic and copies ran while one was open for 8% of the time, Pallas kernels for 0%

commit v1 on v0

v1 whole, which is shorter than its diff:
```python
import jax
import jax.numpy as jnp
from jax import lax
from jax.experimental import pallas as pl
from jax.experimental.pallas import tpu as pltpu
from jax.sharding import PartitionSpec as P

F32 = jnp.float32
LANES = 128
SUBS = 8
STEP = 16
CHUNKS = 4


def make_kernel(rows, group, modes, ctx_size):
    chunk = rows // CHUNKS
    span = rows + STEP

    def kernel(
        q_hbm, k_hbm, v_hbm, r_hbm, d_hbm, g_ref, o_hbm,
        kb, vb, qb, ob, rb, db, xb, rate, fade, amp, ends, heard, starts, enter,
        p_sem, k_sem, v_sem, q_sem, o_sem, e_send, e_recv, s_send, s_recv, t_send, t_recv,
    ):
        half = lax.axis_index("half")
        ctx = lax.axis_index("ctx")
        owner = (half, 1 - half)

        def columns(place):
            return pl.ds(pl.multiple_of(owner[place] * group, group), group)

        def load(hbm, buf, sem, place, c):
            at = pl.ds(c * chunk, chunk)
            return pltpu.make_async_copy(hbm.at[at, columns(place)], buf.at[place, at, :], sem.at[place, c])

        def store(place, c):
            at = pl.ds(c * chunk, chunk)
            return pltpu.make_async_copy(ob.at[place, at, :], o_hbm.at[at, columns(place)], o_sem.at[place, c])

        def remote(src, dst, send_sem, recv_sem, to_half, to_ctx):
            return pltpu.make_async_remote_copy(
                src_ref=src,
                dst_ref=dst,
                send_sem=send_sem,
                recv_sem=recv_sem,
                device_id={"half": to_half, "ctx": to_ctx},
                device_id_type=pl.DeviceIdType.MESH,
            )

        def peer(d):
            return lax.rem(ctx + d, ctx_size)

        def to_owner(d):
            return remote(ends.at[peer(d)], heard.at[ctx], e_send.at[d], e_recv.at[d], half, peer(d))

        def to_same(d):
            return remote(starts.at[peer(d)], enter.at[0, ctx], s_send.at[d], s_recv.at[d], half, peer(d))

        def to_twin(d):
            return remote(starts.at[peer(d)], enter.at[1, ctx], t_send.at[d], t_recv.at[d], 1 - half, peer(d))

        def each(first, act):
            def body(d, carry):
                act(d)
                return carry

            lax.fori_loop(first, ctx_size, body, 0)

        barrier = pltpu.get_barrier_semaphore()

        def greet(to_half):
            def act(d):
                pl.semaphore_signal(
                    barrier,
                    inc=1,
                    device_id={"half": to_half, "ctx": peer(d)},
                    device_id_type=pl.DeviceIdType.MESH,
                )

            return act

        params = [
            pltpu.make_async_copy(src.at[:, columns(place)], dst.at[place], p_sem.at[place, i])
            for place in range(2)
            for i, (src, dst) in enumerate(((d_hbm, db), (r_hbm, rb)))
        ]
        for copy in params:
            copy.start()
        for place in range(2):
            for c in range(CHUNKS):
                load(k_hbm, kb, k_sem, place, c).start()
                load(v_hbm, vb, v_sem, place, c).start()
        for place in range(2):
            for c in range(CHUNKS):
                load(q_hbm, qb, q_sem, place, c).start()
        each(1, greet(half))
        each(0, greet(1 - half))

        def reg(place, m):
            return pl.ds(pl.multiple_of((place * modes + m) * SUBS, SUBS), SUBS)

        def row(place, t):
            return pl.ds(pl.multiple_of((place * span + t) * SUBS, SUBS), SUBS)

        def tile(place, t, b):
            return pl.ds((place * span + t) * SUBS + b, SUBS, stride=SUBS)

        for copy in params:
            copy.wait()
        for place in range(2):
            for b in range(SUBS):
                lanes = pl.ds(b * LANES, LANES)
                for m in range(0, modes, SUBS):
                    d = db[place, m : m + SUBS, lanes]
                    r = rb[place, m : m + SUBS, lanes]
                    at = pl.ds((place * modes + m) * SUBS + b, SUBS, stride=SUBS)
                    rate[at, :] = d
                    fade[at, :] = jnp.exp(-d)
                    amp[at, :] = r * jnp.sqrt(d)

        def arrive(place, c):
            load(k_hbm, kb, k_sem, place, c).wait()
            load(v_hbm, vb, v_sem, place, c).wait()

        def spread(place, t, to):
            for b in range(SUBS):
                lanes = pl.ds(b * LANES, LANES)
                x = kb[place, pl.ds(t, STEP), lanes].astype(F32) * vb[place, pl.ds(t, STEP), lanes].astype(F32)
                for j in range(0, STEP, SUBS):
                    xb[tile(place, to + j, b), :] = x[j : j + SUBS]

        zeros = jnp.zeros((SUBS, LANES), F32)

        held = (zeros,) * modes
        for c in range(CHUNKS):
            first = c * chunk
            arrive(0, c)
            spread(0, first, first)

            def gather(i, held, first=first):
                t = pl.multiple_of(first + i * STEP, STEP)
                xs = [xb[row(0, t + j), :] for j in range(STEP)]
                held = list(held)
                for m in range(modes):
                    a = fade[reg(0, m), :]
                    for x in xs:
                        held[m] = held[m] * a + x
                spread(0, pl.multiple_of(jnp.minimum(t + STEP, first + chunk - STEP), STEP), t + STEP)
                return tuple(held)

            held = lax.fori_loop(0, chunk // STEP, gather, held)
        for m in range(modes):
            ends[m] = held[m]

        pl.semaphore_wait(barrier, 2 * ctx_size - 1)
        each(1, lambda d: to_owner(d).start())

        def respond(place, look):
            g = g_ref[pl.ds(pl.multiple_of(owner[place] * SUBS, SUBS), SUBS), :]

            def body(i, held):
                t = pl.multiple_of(i * STEP, STEP)
                held = list(held)
                for s in range(0, STEP, SUBS):
                    xs = [xb[row(place, t + s + j), :] for j in range(SUBS)]
                    ys = [g * x for x in xs]
                    for m in range(modes):
                        a = fade[reg(place, m), :]
                        w = amp[reg(place, m), :]
                        for j in range(SUBS):
                            held[m] = held[m] * a + xs[j]
                            ys[j] = ys[j] + w * held[m]
                    for j in range(SUBS):
                        xb[row(place, t + s + j), :] = ys[j]
                if look:
                    spread(place, pl.multiple_of(jnp.minimum(t + STEP, rows - STEP), STEP), t + STEP)
                return tuple(held)

            lax.fori_loop(0, rows // STEP, body, (zeros,) * modes)

        respond(0, False)

        heard[ctx] = ends[ctx]
        each(1, lambda d: to_owner(d).wait())
        whole = jnp.exp(-float(rows) * rate[reg(0, ctx), :])
        state = zeros
        for j in range(ctx_size):
            starts[j] = state
            state = state * whole + heard[j]
        each(1, lambda d: to_same(d).start())
        each(0, lambda d: to_twin(d).start())

        for c in range(CHUNKS):
            arrive(1, c)
        spread(1, 0, 0)
        respond(1, True)

        enter[0, ctx] = starts[ctx]
        each(1, lambda d: to_same(d).wait())
        each(0, lambda d: to_twin(d).wait())

        for place in range(2):
            state = tuple(amp[reg(place, m), :] * enter[place, m] for m in range(modes))
            for c in range(CHUNKS):
                load(q_hbm, qb, q_sem, place, c).wait()

                def finish(i, state, place=place, first=c * chunk):
                    t = pl.multiple_of(first + i * STEP, STEP)
                    state = list(state)
                    for s in range(0, STEP, SUBS):
                        ys = [xb[row(place, t + s + j), :] for j in range(SUBS)]
                        for m in range(modes):
                            a = fade[reg(place, m), :]
                            for j in range(SUBS):
                                state[m] = state[m] * a
                                ys[j] = ys[j] + state[m]
                        for j in range(SUBS):
                            xb[row(place, t + s + j), :] = ys[j]
                    for b in range(SUBS):
                        lanes = pl.ds(b * LANES, LANES)
                        y = jnp.concatenate([xb[tile(place, t + j, b), :] for j in range(0, STEP, SUBS)])
                        gate = qb[place, pl.ds(t, STEP), lanes].astype(F32)
                        ob[place, pl.ds(t, STEP), lanes] = (gate * y).astype(jnp.bfloat16)
                    return tuple(state)

                state = lax.fori_loop(0, chunk // STEP, finish, state)
                store(place, c).start()
        for place in range(2):
            for c in range(CHUNKS):
                store(place, c).wait()

    return kernel


def shards(query_gate, key_gate, value_input, residues, decays, skip_gain):
    rows, width = key_gate.shape
    modes = residues.shape[0]
    group = width // 2
    ctx_size = lax.axis_size("ctx")
    assert group == SUBS * LANES and modes == ctx_size
    wide = (2, rows, group)
    register = (SUBS, LANES)
    dma = pltpu.SemaphoreType.DMA
    anywhere = pl.BlockSpec(memory_space=pl.ANY)
    return pl.pallas_call(
        make_kernel(rows, group, modes, ctx_size),
        out_shape=jax.ShapeDtypeStruct((rows, width), jnp.bfloat16),
        in_specs=[anywhere] * 5 + [pl.BlockSpec(memory_space=pltpu.VMEM)],
        out_specs=anywhere,
        scratch_shapes=[
            pltpu.VMEM(wide, jnp.bfloat16),
            pltpu.VMEM(wide, jnp.bfloat16),
            pltpu.VMEM(wide, jnp.bfloat16),
            pltpu.VMEM(wide, jnp.bfloat16),
            pltpu.VMEM((2, modes, group), F32),
            pltpu.VMEM((2, modes, group), F32),
            pltpu.VMEM((2 * (rows + STEP) * SUBS, LANES), F32),
            pltpu.VMEM((2 * modes * SUBS, LANES), F32),
            pltpu.VMEM((2 * modes * SUBS, LANES), F32),
            pltpu.VMEM((2 * modes * SUBS, LANES), F32),
            pltpu.VMEM((modes, *register), F32),
            pltpu.VMEM((ctx_size, *register), F32),
            pltpu.VMEM((ctx_size, *register), F32),
            pltpu.VMEM((2, modes, *register), F32),
            dma((2, 2)),
            dma((2, CHUNKS)),
            dma((2, CHUNKS)),
            dma((2, CHUNKS)),
            dma((2, CHUNKS)),
        ]
        + [dma((ctx_size,))] * 6,
        compiler_params=pltpu.CompilerParams(
            collective_id=0, has_side_effects=True, vmem_limit_bytes=48 << 20
        ),
    )(query_gate, key_gate, value_input, residues, decays, skip_gain.reshape(2 * SUBS, LANES))


def solution(mesh):
    placed = (
        P("ctx", "chan"),
        P("ctx", "chan"),
        P("ctx", "chan"),
        P(None, "chan"),
        P(None, "chan"),
        P("chan"),
    )
    return jax.shard_map(shards, mesh=mesh, in_specs=placed, out_specs=P("ctx", "chan"), check_vma=False)
```

time: 723 us -> 31.5 us (0.04)
  the two profiles are of different devices: /device:TPU:96 before, /device:TPU:1 now
where the time goes in v1:
time: 31.5 us; the launch traced here: 31.3 us
  Pallas kernels  25.9 us (82%)
  local copies, waits for them, and re-layouts  5.42 us (17%)
    pallas_call x1, Pallas kernels, shards(): pl.pallas_call(make_kernel(rows, group, modes, ctx_size), out_shape=jax.S...  25.9 us
    unnamed x9, local copies, waits for them, and re-layouts  5.42 us

profile of v1, /device:TPU:1, one launch (start us, length us, event | category | flops | bytes accessed | tf_op | source)
XLA Modules:
  0.0 31.3 jit_solution(7875427276069865175)
XLA Ops:
  0.0 0.0 copy-start
  0.0 1.6 %copy-done = bf16[512,2048]{1,0:T(8,128)(2,1)S(1)} copy-done((bf16[512,2048]{1,0:T(8,128)(2,1)S(1)}, bf16[512,2048]{1,0:T(8,128)(2,1)}, u32[]{:S(2)}) %copy-start) | copy-done | bytes 2097176
  1.6 0.0 copy-start.1
  1.6 0.9 %copy-done.1 = f32[16,2048]{1,0:T(8,128)S(1)} copy-done((f32[16,2048]{1,0:T(8,128)S(1)}, f32[16,2048]{1,0:T(8,128)}, u32[]{:S(2)}) %copy-start.1) | copy-done | bytes 131096
  2.5 0.0 copy-start.2
  2.5 0.9 %copy-done.2 = f32[16,2048]{1,0:T(8,128)S(1)} copy-done((f32[16,2048]{1,0:T(8,128)S(1)}, f32[16,2048]{1,0:T(8,128)}, u32[]{:S(2)}) %copy-start.2) | copy-done | bytes 131096
  3.4 0.0 copy-start.3
  3.4 0.7 %copy-done.3 = f32[2048]{0:T(1024)S(1)} copy-done((f32[2048]{0:T(1024)S(1)}, f32[2048]{0:T(1024)}, u32[]{:S(2)}) %copy-start.3) | copy-done | bytes 8216
  4.1 25.9 %shard_map.64 = bf16[512,2048]{1,0:T(8,128)(2,1)S(1)} custom-call(bf16[512,2048]{1,0:T(8,128)(2,1)S(1)} %copy-done, bf16[512,2048]{1,0:T(8,128)(2,1)} %k_hbm.1, bf16[512,2048]{1,0:T(8,128)(2,1)} %v_hbm.1, f32[16,2048]{1,0:T(8,128)S(1)} %copy-done.1, f32[16,2048]{1,0:T(8,128)S(1)} %copy-done.2, f32[16,128]{1,0:T(8,128)S(1)} %bitcast.1), custom_call_target="tpu_custom_call" | custom-call | tf_op jit(solution)/shard_map/pallas_call | solution.py:244
  30.0 1.3 %copy.8 = bf16[512,2048]{1,0:T(8,128)(2,1)} copy(bf16[512,2048]{1,0:T(8,128)(2,1)S(1)} %shard_map.64) | data formatting | bytes 4194304
Async XLA Ops:
  0.0 1.6 %copy-start = (bf16[512,2048]{1,0:T(8,128)(2,1)S(1)}, bf16[512,2048]{1,0:T(8,128)(2,1)}, u32[]{:S(2)}) copy-start(bf16[512,2048]{1,0:T(8,128)(2,1)} %q_hbm.1) | copy-start | bytes 6291460
  1.6 0.9 %copy-start.1 = (f32[16,2048]{1,0:T(8,128)S(1)}, f32[16,2048]{1,0:T(8,128)}, u32[]{:S(2)}) copy-start(f32[16,2048]{1,0:T(8,128)} %r_hbm.1) | copy-start | bytes 393220
  2.5 0.9 %copy-start.2 = (f32[16,2048]{1,0:T(8,128)S(1)}, f32[16,2048]{1,0:T(8,128)}, u32[]{:S(2)}) copy-start(f32[16,2048]{1,0:T(8,128)} %d_hbm.1) | copy-start | bytes 393220
  3.4 0.7 %copy-start.3 = (f32[2048]{0:T(1024)S(1)}, f32[2048]{0:T(1024)}, u32[]{:S(2)}) copy-start(f32[2048]{0:T(1024)} %param.11) | copy-start | bytes 24580

commit v2 on v1

v2 whole, which is shorter than its diff:
```python
import jax
import jax.numpy as jnp
from jax import lax
from jax.experimental import pallas as pl
from jax.experimental.pallas import tpu as pltpu
from jax.sharding import PartitionSpec as P

F32 = jnp.float32
LANES = 128
SUBS = 8
TILE = 16
BLOCK = 8
STEP = 32
CHUNKS = 4
SIDE = 4


def torus(d):
    return sum(min(c, SIDE - c) for c in d)


OFFSETS = sorted(((a, b) for a in range(SIDE) for b in range(SIDE)), key=torus, reverse=True)
BACK = [OFFSETS.index((-a % SIDE, -b % SIDE)) for a, b in OFFSETS]
MODES = len(OFFSETS)
FAR = [n for n in range(MODES) if torus(OFFSETS[n]) > 2]
MID = [n for n in range(MODES) if torus(OFFSETS[n]) == 2]
NEAR = [n for n in range(MODES) if torus(OFFSETS[n]) < 2]
SELF = MODES - 1


def make_kernel(rows, group):
    chunk = rows // CHUNKS
    span = rows + STEP

    def kernel(
        q_hbm, k_hbm, v_hbm, r_hbm, d_hbm, g_hbm, o_hbm,
        kb, vb, qb, ob, rb, db, gb, xb, rate, raw, fade, fade8, amp, taps, left, ends, heard, starts, enter,
        p_sem, k_sem, v_sem, q_sem, o_sem, e_send, e_recv, s_send, s_recv, t_send, t_recv,
    ):
        half = lax.axis_index("half")
        ctx = lax.axis_index("ctx")
        owner = (half, 1 - half)

        def columns(place):
            return pl.ds(pl.multiple_of(owner[place] * group, group), group)

        def load(hbm, buf, sem, place, c):
            at = pl.ds(c * chunk, chunk)
            return pltpu.make_async_copy(hbm.at[at, columns(place)], buf.at[place, at, :], sem.at[place, c])

        def store(place, c):
            at = pl.ds(c * chunk, chunk)
            return pltpu.make_async_copy(ob.at[place, at, :], o_hbm.at[at, columns(place)], o_sem.at[place, c])

        def remote(src, dst, send_sem, recv_sem, to_half, to_ctx):
            return pltpu.make_async_remote_copy(
                src_ref=src,
                dst_ref=dst,
                send_sem=send_sem,
                recv_sem=recv_sem,
                device_id={"half": to_half, "ctx": to_ctx},
                device_id_type=pl.DeviceIdType.MESH,
            )

        def peer(n):
            a, b = OFFSETS[n]
            return lax.rem(ctx // SIDE + a, SIDE) * SIDE + lax.rem(lax.rem(ctx, SIDE) + b, SIDE)

        def to_owner(n):
            return remote(ends.at[n], heard.at[ctx], e_send.at[n], e_recv.at[n], half, peer(n))

        def to_same(n):
            return remote(starts.at[peer(n)], enter.at[0, BACK[n]], s_send.at[n], s_recv.at[n], half, peer(n))

        def to_twin(n):
            return remote(starts.at[peer(n)], enter.at[1, BACK[n]], t_send.at[n], t_recv.at[n], 1 - half, peer(n))

        barrier = pltpu.get_barrier_semaphore()

        def greet(to_half, to_ctx):
            pl.semaphore_signal(
                barrier, inc=1, device_id={"half": to_half, "ctx": to_ctx}, device_id_type=pl.DeviceIdType.MESH
            )

        params = [
            pltpu.make_async_copy(src.at[:, columns(place)], dst.at[place], p_sem.at[place, i])
            for place in range(2)
            for i, (src, dst) in enumerate(((d_hbm, db), (r_hbm, rb)))
        ]
        params += [
            pltpu.make_async_copy(
                g_hbm.at[pl.ds(pl.multiple_of(owner[place] * SUBS, SUBS), SUBS), :], gb.at[place], p_sem.at[place, 2]
            )
            for place in range(2)
        ]
        for copy in params:
            copy.start()
        for place in range(2):
            for c in range(CHUNKS):
                load(k_hbm, kb, k_sem, place, c).start()
                load(v_hbm, vb, v_sem, place, c).start()
        for place in range(2):
            for c in range(CHUNKS):
                load(q_hbm, qb, q_sem, place, c).start()
        for n in range(MODES):
            if n != SELF:
                greet(half, peer(n))
            greet(1 - half, peer(n))

        def reg(place, n):
            return pl.ds(pl.multiple_of((place * MODES + n) * SUBS, SUBS), SUBS)

        def row(place, t):
            return pl.ds(pl.multiple_of((place * span + t) * SUBS, SUBS), SUBS)

        def tile(place, t, b):
            return pl.ds((place * span + t) * SUBS + b, SUBS, stride=SUBS)

        for copy in params:
            copy.wait()
        for place in range(2):
            for b in range(SUBS):
                lanes = pl.ds(b * LANES, LANES)
                for m in range(0, MODES, SUBS):
                    at = pl.ds((place * MODES + m) * SUBS + b, SUBS, stride=SUBS)
                    rate[at, :] = db[place, m : m + SUBS, lanes]
                    raw[at, :] = rb[place, m : m + SUBS, lanes]
        for place in range(2):
            for n in range(MODES):
                d = rate[reg(place, peer(n)), :]
                a = jnp.exp(-d)
                fade[reg(place, n), :] = a
                fade8[reg(place, n), :] = jnp.exp(-float(BLOCK) * d)
                amp[reg(place, n), :] = raw[reg(place, peer(n)), :] * jnp.sqrt(d)

        def make_taps(place):
            terms = [amp[reg(place, n), :] for n in range(MODES)]
            for j in range(BLOCK):
                total = sum(terms[1:], terms[0])
                taps[reg(place, j), :] = total + gb[place] if j == 0 else total
                terms = [term * fade[reg(place, n), :] for n, term in enumerate(terms)]
            for n in range(MODES):
                amp[reg(place, n), :] = amp[reg(place, n), :] * fade[reg(place, n), :]

        def arrive(place, c):
            load(k_hbm, kb, k_sem, place, c).wait()
            load(v_hbm, vb, v_sem, place, c).wait()

        def spread(place, t, to):
            for b in range(SUBS):
                lanes = pl.ds(b * LANES, LANES)
                for i in range(0, STEP, TILE):
                    at = pl.ds(t + i, TILE)
                    x = kb[place, at, lanes].astype(F32) * vb[place, at, lanes].astype(F32)
                    for j in range(0, TILE, SUBS):
                        xb[tile(place, to + i + j, b), :] = x[j : j + SUBS]

        def read(place, t):
            return [xb[row(place, t + j), :] for j in range(BLOCK)]

        def leave(xs, a):
            held = xs[0]
            for x in xs[1:]:
                held = held * a + x
            return held

        def answer(place, t, xs):
            for j in reversed(range(BLOCK)):
                y = taps[reg(place, 0), :] * xs[j]
                for i in range(j):
                    y = y + taps[reg(place, j - i), :] * xs[i]
                xb[row(place, t + j), :] = y

        def gather(slots, look, first, size, held):
            def body(i, held):
                t = pl.multiple_of(first + i * STEP, STEP)
                held = list(held)
                for s in range(0, STEP, BLOCK):
                    xs = read(0, t + s)
                    for at, n in enumerate(slots):
                        e = leave(xs, fade[reg(0, n), :])
                        left[0, (t + s) // BLOCK, n] = e
                        held[at] = held[at] * fade8[reg(0, n), :] + e
                if look:
                    spread(0, pl.multiple_of(jnp.minimum(t + STEP, first + size - STEP), STEP), t + STEP)
                return tuple(held)

            return lax.fori_loop(0, size // STEP, body, held)

        zeros = jnp.zeros((SUBS, LANES), F32)
        held = (zeros,) * len(FAR)
        for c in range(CHUNKS):
            arrive(0, c)
            spread(0, c * chunk, c * chunk)
            held = gather(FAR, True, c * chunk, chunk, held)
        for at, n in enumerate(FAR):
            ends[n] = held[at]
        held = gather(MID, False, 0, rows, (zeros,) * len(MID))
        for at, n in enumerate(MID):
            ends[n] = held[at]

        pl.semaphore_wait(barrier, 2 * MODES - 1)
        for n in FAR + MID:
            to_owner(n).start()
        held = gather(NEAR, False, 0, rows, (zeros,) * len(NEAR))
        for at, n in enumerate(NEAR):
            ends[n] = held[at]
        for n in NEAR:
            if n != SELF:
                to_owner(n).start()

        make_taps(0)
        make_taps(1)

        def own(i, carry):
            t = pl.multiple_of(i * STEP, STEP)
            for s in range(0, STEP, BLOCK):
                answer(0, t + s, read(0, t + s))
            return carry

        lax.fori_loop(0, rows // STEP, own, 0)

        def other(i, carry):
            t = pl.multiple_of(i * STEP, STEP)
            for s in range(0, STEP, BLOCK):
                xs = read(1, t + s)
                for n in range(MODES):
                    left[1, (t + s) // BLOCK, n] = leave(xs, fade[reg(1, n), :])
                answer(1, t + s, xs)
            spread(1, pl.multiple_of(jnp.minimum(t + STEP, rows - STEP), STEP), t + STEP)
            return carry

        for c in range(CHUNKS):
            arrive(1, c)
        spread(1, 0, 0)
        part = rows // STEP * 5 // 8
        lax.fori_loop(0, part, other, 0)

        heard[ctx] = ends[SELF]
        for n in range(MODES):
            if n != SELF:
                to_owner(n).wait()
        whole = jnp.exp(-float(rows) * rate[reg(0, ctx), :])
        state = zeros
        for j in range(MODES):
            starts[j] = state
            state = state * whole + heard[j]
        for n in range(MODES):
            if n != SELF:
                to_same(n).start()
            to_twin(n).start()
        enter[0, SELF] = starts[ctx]

        lax.fori_loop(part, rows // STEP, other, 0)

        def pour(place, slots, first, size, last, state):
            def body(i, state):
                t = pl.multiple_of(first + i * STEP, STEP)
                state = list(state)
                for s in range(0, STEP, BLOCK):
                    ys = read(place, t + s)
                    for at, n in enumerate(slots):
                        a = fade[reg(place, n), :]
                        now = state[at] * amp[reg(place, n), :]
                        ys[0] = ys[0] + now
                        for j in range(1, BLOCK):
                            now = now * a
                            ys[j] = ys[j] + now
                        state[at] = state[at] * fade8[reg(place, n), :] + left[place, (t + s) // BLOCK, n]
                    for j in range(BLOCK):
                        xb[row(place, t + s + j), :] = ys[j]
                if last:
                    for b in range(SUBS):
                        lanes = pl.ds(b * LANES, LANES)
                        for i in range(0, STEP, TILE):
                            at = pl.ds(t + i, TILE)
                            y = jnp.concatenate([xb[tile(place, t + i + j, b), :] for j in range(0, TILE, SUBS)])
                            ob[place, at, lanes] = (qb[place, at, lanes].astype(F32) * y).astype(jnp.bfloat16)
                return tuple(state)

            return lax.fori_loop(0, size // STEP, body, state)

        for slots in (NEAR, MID):
            for place in range(2):
                for n in slots:
                    if place == 0 and n != SELF:
                        to_same(BACK[n]).wait()
                    if place == 1:
                        to_twin(BACK[n]).wait()
                pour(place, slots, 0, rows, False, tuple(enter[place, n] for n in slots))
        for place in range(2):
            for n in FAR:
                if place == 0:
                    to_same(BACK[n]).wait()
                else:
                    to_twin(BACK[n]).wait()
            state = tuple(enter[place, n] for n in FAR)
            for c in range(CHUNKS):
                load(q_hbm, qb, q_sem, place, c).wait()
                state = pour(place, FAR, c * chunk, chunk, True, state)
                store(place, c).start()
        for place in range(2):
            for c in range(CHUNKS):
                store(place, c).wait()

    return kernel


def shards(query_gate, key_gate, value_input, residues, decays, skip_gain):
    rows, width = key_gate.shape
    group = width // 2
    assert group == SUBS * LANES and residues.shape[0] == MODES == lax.axis_size("ctx")
    wide = (2, rows, group)
    register = (SUBS, LANES)
    dma = pltpu.SemaphoreType.DMA
    hbm = pl.BlockSpec(memory_space=pltpu.HBM)
    return pl.pallas_call(
        make_kernel(rows, group),
        out_shape=jax.ShapeDtypeStruct((rows, width), jnp.bfloat16),
        in_specs=[hbm] * 6,
        out_specs=hbm,
        scratch_shapes=[pltpu.VMEM(wide, jnp.bfloat16)] * 4
        + [pltpu.VMEM((2, MODES, group), F32)] * 2
        + [
            pltpu.VMEM((2, *register), F32),
            pltpu.VMEM((2 * (rows + STEP) * SUBS, LANES), F32),
        ]
        + [pltpu.VMEM((2 * MODES * SUBS, LANES), F32)] * 6
        + [pltpu.VMEM((2, rows // BLOCK, MODES, *register), F32)]
        + [pltpu.VMEM((MODES, *register), F32)] * 3
        + [
            pltpu.VMEM((2, MODES, *register), F32),
            dma((2, 3)),
        ]
        + [dma((2, CHUNKS))] * 4
        + [dma((MODES,))] * 6,
        compiler_params=pltpu.CompilerParams(
            collective_id=0, has_side_effects=True, vmem_limit_bytes=67_043_328
        ),
    )(query_gate, key_gate, value_input, residues, decays, skip_gain.reshape(2 * SUBS, LANES))


def solution(mesh):
    placed = (
        P("ctx", "chan"),
        P("ctx", "chan"),
        P("ctx", "chan"),
        P(None, "chan"),
        P(None, "chan"),
        P("chan"),
    )
    return jax.shard_map(shards, mesh=mesh, in_specs=placed, out_specs=P("ctx", "chan"), check_vma=False)
```

time: 31.5 us -> 28.4 us (0.902)
  the two profiles are of different devices: /device:TPU:1 before, /device:TPU:0 now
where the time goes in v2:
time: 28.4 us; the launch traced here: 28.3 us
  Pallas kernels  25.1 us (88%)
  local copies, waits for them, and re-layouts  3.16 us (11%)
    pallas_call x1, Pallas kernels, shards(): pl.pallas_call(make_kernel(rows, group), out_shape=jax.ShapeDtypeStruct((...  25.1 us
    unnamed x1, local copies, waits for them, and re-layouts  3.16 us

profile of v2, /device:TPU:0, one launch (start us, length us, event | category | flops | bytes accessed | tf_op | source)
XLA Modules:
  0.0 28.3 jit_solution(5897024701929485272)
XLA Ops:
  0.0 25.1 %shard_map.64 = bf16[512,2048]{1,0:T(8,128)(2,1)} custom-call(bf16[512,2048]{1,0:T(8,128)(2,1)} %q_hbm.1, bf16[512,2048]{1,0:T(8,128)(2,1)} %k_hbm.1, bf16[512,2048]{1,0:T(8,128)(2,1)} %v_hbm.1, f32[16,2048]{1,0:T(8,128)} %r_hbm.1, f32[16,2048]{1,0:T(8,128)} %d_hbm.1, f32[16,128]{1,0:T(8,128)} %bitcast.1), custom_call_target="tpu_custom_call" | custom-call | tf_op jit(solution)/shard_map/pallas_call | solution.py:317
  25.2 3.2 %copy.8 = bf16[512,2048]{1,0:T(8,128)(2,1)} copy(bf16[512,2048]{1,0:T(8,128)(2,1)} %shard_map.64) | data formatting | bytes 4194304

commit v3 on v2

--- a/solution.py
+++ b/solution.py
@@ -11,6 +11,7 @@
 TILE = 16
 BLOCK = 8
 STEP = 32
+SPAN = 512 + STEP
 CHUNKS = 4
 SIDE = 4
 
@@ -28,14 +29,55 @@
 SELF = MODES - 1
 
 
-def make_kernel(rows, group):
+def reg(place, n):
+    return pl.ds(pl.multiple_of((place * MODES + n) * SUBS, SUBS), SUBS)
+
+
+def row(place, t):
+    return pl.ds(pl.multiple_of((place * SPAN + t) * SUBS, SUBS), SUBS)
+
+
+def tile(place, t, b):
+    return pl.ds((place * SPAN + t) * SUBS + b, SUBS, stride=SUBS)
+
+
+def pour(place, slots, first, size, refs, state, then=None):
+    xb, left, fade, fade8, amp = refs
+
+    def body(i, state):
+        t = pl.multiple_of(first + i * STEP, STEP)
+        state = list(state)
+        for s in range(0, STEP, BLOCK):
+            ys = [xb[row(place, t + s + j), :] for j in range(BLOCK)]
+            for at, n in enumerate(slots):
+                a = fade[reg(place, n), :]
+                now = state[at] * amp[reg(place, n), :]
+                ys[0] = ys[0] + now
+                for j in range(1, BLOCK):
+                    now = now * a
+                    ys[j] = ys[j] + now
+                state[at] = state[at] * fade8[reg(place, n), :] + left[place, (t + s) // BLOCK, n]
+            for j in range(BLOCK):
+                xb[row(place, t + s + j), :] = ys[j]
+        if then is not None:
+            then(t)
+        return tuple(state)
+
+    return lax.fori_loop(0, size // STEP, body, state)
+
+
+FIRST_VMEM = 40 << 20
+SECOND_VMEM = 40 << 20
+
+
+def make_first(rows, group):
     chunk = rows // CHUNKS
-    span = rows + STEP
+    assert SPAN == rows + STEP
 
     def kernel(
-        q_hbm, k_hbm, v_hbm, r_hbm, d_hbm, g_hbm, o_hbm,
-        kb, vb, qb, ob, rb, db, gb, xb, rate, raw, fade, fade8, amp, taps, left, ends, heard, starts, enter,
-        p_sem, k_sem, v_sem, q_sem, o_sem, e_send, e_recv, s_send, s_recv, t_send, t_recv,
+        k_hbm, v_hbm, r_hbm, d_hbm, g_hbm, xb, left, enter, fade, fade8, amp,
+        kb, vb, rb, db, gb, rate, raw, taps, ends, heard, starts,
+        p_sem, k_sem, v_sem, e_send, e_recv, s_send, s_recv, t_send, t_recv,
     ):
         half = lax.axis_index("half")
         ctx = lax.axis_index("ctx")
@@ -47,10 +89,6 @@
         def load(hbm, buf, sem, place, c):
             at = pl.ds(c * chunk, chunk)
             return pltpu.make_async_copy(hbm.at[at, columns(place)], buf.at[place, at, :], sem.at[place, c])
-
-        def store(place, c):
-            at = pl.ds(c * chunk, chunk)
-            return pltpu.make_async_copy(ob.at[place, at, :], o_hbm.at[at, columns(place)], o_sem.at[place, c])
 
         def remote(src, dst, send_sem, recv_sem, to_half, to_ctx):
             return pltpu.make_async_remote_copy(
@@ -99,22 +137,10 @@
             for c in range(CHUNKS):
                 load(k_hbm, kb, k_sem, place, c).start()
                 load(v_hbm, vb, v_sem, place, c).start()
-        for place in range(2):
-            for c in range(CHUNKS):
-                load(q_hbm, qb, q_sem, place, c).start()
         for n in range(MODES):
             if n != SELF:
                 greet(half, peer(n))
             greet(1 - half, peer(n))
-
-        def reg(place, n):
-            return pl.ds(pl.multiple_of((place * MODES + n) * SUBS, SUBS), SUBS)
-
-        def row(place, t):
-            return pl.ds(pl.multiple_of((place * span + t) * SUBS, SUBS), SUBS)
-
-        def tile(place, t, b):
-            return pl.ds((place * span + t) * SUBS + b, SUBS, stride=SUBS)
 
         for copy in params:
             copy.wait()
@@ -253,33 +279,6 @@
 
         lax.fori_loop(part, rows // STEP, other, 0)
 
-        def pour(place, slots, first, size, last, state):
-            def body(i, state):
-                t = pl.multiple_of(first + i * STEP, STEP)
-                state = list(state)
-                for s in range(0, STEP, BLOCK):
-                    ys = read(place, t + s)
-                    for at, n in enumerate(slots):
-                        a = fade[reg(place, n), :]
-                        now = state[at] * amp[reg(place, n), :]
-                        ys[0] = ys[0] + now
-                        for j in range(1, BLOCK):
-                            now = now * a
-                            ys[j] = ys[j] + now
-                        state[at] = state[at] * fade8[reg(place, n), :] + left[place, (t + s) // BLOCK, n]
-                    for j in range(BLOCK):
-                        xb[row(place, t + s + j), :] = ys[j]
-                if last:
-                    for b in range(SUBS):
-                        lanes = pl.ds(b * LANES, LANES)
-                        for i in range(0, STEP, TILE):
-                            at = pl.ds(t + i, TILE)
-                            y = jnp.concatenate([xb[tile(place, t + i + j, b), :] for j in range(0, TILE, SUBS)])
-                            ob[place, at, lanes] = (qb[place, at, lanes].astype(F32) * y).astype(jnp.bfloat16)
-                return tuple(state)
-
-            return lax.fori_loop(0, size // STEP, body, state)
-
         for slots in (NEAR, MID):
             for place in range(2):
                 for n in slots:
@@ -287,17 +286,72 @@
                         to_same(BACK[n]).wait()
                     if place == 1:
                         to_twin(BACK[n]).wait()
-                pour(place, slots, 0, rows, False, tuple(enter[place, n] for n in slots))
-        for place in range(2):
-            for n in FAR:
-                if place == 0:
-                    to_same(BACK[n]).wait()
-                else:
-                    to_twin(BACK[n]).wait()
+                state = tuple(enter[place, n] for n in slots)
+                pour(place, slots, 0, rows, (xb, left, fade, fade8, amp), state)
+        for n in FAR:
+            to_same(BACK[n]).wait()
+            to_twin(BACK[n]).wait()
+
+    return kernel
+
+
+def finish(place, first, size, state, refs, qb, ob):
+    xs, xb, left, fade, fade8, amp = refs
+
+    def body(i, state):
+        t = pl.multiple_of(first + i * STEP, STEP)
+        state = list(state)
+        for s in range(0, STEP, BLOCK):
+            ys = [xs[row(place, t + s + j), :] for j in range(BLOCK)]
+            for at, n in enumerate(FAR):
+                a = fade[reg(place, n), :]
+                now = state[at] * amp[reg(place, n), :]
+                ys[0] = ys[0] + now
+                for j in range(1, BLOCK):
+                    now = now * a
+                    ys[j] = ys[j] + now
+                state[at] = state[at] * fade8[reg(place, n), :] + left[place, (t + s) // BLOCK, n]
+            for j in range(BLOCK):
+                xb[pl.ds((s + j) * SUBS, SUBS), :] = ys[j]
+        for b in range(SUBS):
+            lanes = pl.ds(b * LANES, LANES)
+            for i in range(0, STEP, TILE):
+                at = pl.ds(t + i, TILE)
+                y = jnp.concatenate(
+                    [xb[pl.ds((i + j) * SUBS + b, SUBS, stride=SUBS), :] for j in range(0, TILE, SUBS)]
+                )
+                ob[place, at, lanes] = (qb[place, at, lanes].astype(F32) * y).astype(jnp.bfloat16)
+        return tuple(state)
+
+    return lax.fori_loop(0, size // STEP, body, state)
+
+
+def make_second(rows, group):
+    chunk = rows // CHUNKS
+
+    def kernel(q_hbm, xs, left, enter, fade, fade8, amp, o_hbm, xb, qb, ob, q_sem, o_sem):
+        half = lax.axis_index("half")
+        owner = (half, 1 - half)
+
+        def columns(place):
+            return pl.ds(pl.multiple_of(owner[place] * group, group), group)
+
+        def load(place, c):
+            at = pl.ds(c * chunk, chunk)
+            return pltpu.make_async_copy(q_hbm.at[at, columns(place)], qb.at[place, at, :], q_sem.at[place, c])
+
+        def store(place, c):
+            at = pl.ds(c * chunk, chunk)
+            return pltpu.make_async_copy(ob.at[place, at, :], o_hbm.at[at, columns(place)], o_sem.at[place, c])
+
+        for place in range(2):
+            for c in range(CHUNKS):
+                load(place, c).start()
+        for place in range(2):
             state = tuple(enter[place, n] for n in FAR)
             for c in range(CHUNKS):
-                load(q_hbm, qb, q_sem, place, c).wait()
-                state = pour(place, FAR, c * chunk, chunk, True, state)
+                load(place, c).wait()
+                state = finish(place, c * chunk, chunk, state, (xs, xb, left, fade, fade8, amp), qb, ob)
                 store(place, c).start()
         for place in range(2):
             for c in range(CHUNKS):
@@ -314,30 +368,43 @@
     register = (SUBS, LANES)
     dma = pltpu.SemaphoreType.DMA
     hbm = pl.BlockSpec(memory_space=pltpu.HBM)
-    return pl.pallas_call(
-        make_kernel(rows, group),
-        out_shape=jax.ShapeDtypeStruct((rows, width), jnp.bfloat16),
-        in_specs=[hbm] * 6,
-        out_specs=hbm,
-        scratch_shapes=[pltpu.VMEM(wide, jnp.bfloat16)] * 4
+    vmem = pl.BlockSpec(memory_space=pltpu.VMEM)
+    table = (2 * MODES * SUBS, LANES)
+    between = [
+        (2 * SPAN * SUBS, LANES),
+        (2, rows // BLOCK, MODES, *register),
+        (2, MODES, *register),
+        table,
+        table,
+        table,
+    ]
+    kept = pl.pallas_call(
+        make_first(rows, group),
+        out_shape=[jax.ShapeDtypeStruct(shape, F32) for shape in between],
+        in_specs=[hbm] * 5,
+        out_specs=[vmem] * len(between),
+        scratch_shapes=[pltpu.VMEM(wide, jnp.bfloat16)] * 2
         + [pltpu.VMEM((2, MODES, group), F32)] * 2
-        + [
-            pltpu.VMEM((2, *register), F32),
-            pltpu.VMEM((2 * (rows + STEP) * SUBS, LANES), F32),
-        ]
-        + [pltpu.VMEM((2 * MODES * SUBS, LANES), F32)] * 6
-        + [pltpu.VMEM((2, rows // BLOCK, MODES, *register), F32)]
+        + [pltpu.VMEM((2, *register), F32)]
+        + [pltpu.VMEM(table, F32)] * 3
         + [pltpu.VMEM((MODES, *register), F32)] * 3
-        + [
-            pltpu.VMEM((2, MODES, *register), F32),
-            dma((2, 3)),
-        ]
-        + [dma((2, CHUNKS))] * 4
+        + [dma((2, 3))]
+        + [dma((2, CHUNKS))] * 2
         + [dma((MODES,))] * 6,
         compiler_params=pltpu.CompilerParams(
-            collective_id=0, has_side_effects=True, vmem_limit_bytes=67_043_328
+            collective_id=0, has_side_effects=True, vmem_limit_bytes=FIRST_VMEM
         ),
-    )(query_gate, key_gate, value_input, residues, decays, skip_gain.reshape(2 * SUBS, LANES))
+    )(*(pltpu.with_memory_space_constraint(x, pltpu.HBM) for x in (key_gate, value_input, residues, decays, skip_gain.reshape(2 * SUBS, LANES))))
+    return pl.pallas_call(
+        make_second(rows, group),
+        out_shape=jax.ShapeDtypeStruct((rows, width), jnp.bfloat16),
+        in_specs=[hbm] + [vmem] * len(between),
+        out_specs=hbm,
+        scratch_shapes=[pltpu.VMEM((STEP * SUBS, LANES), F32)]
+        + [pltpu.VMEM(wide, jnp.bfloat16)] * 2
+        + [dma((2, CHUNKS))] * 2,
+        compiler_params=pltpu.CompilerParams(vmem_limit_bytes=SECOND_VMEM),
+    )(pltpu.with_memory_space_constraint(query_gate, pltpu.HBM), *kept)
 
 
 def solution(mesh):

time: 28.4 us -> 25.6 us (0.901)
  local copies, waits for them, and re-layouts: 3.16 us -> 0 us
  Pallas kernels: 25.1 us -> 25.5 us
    unnamed x1 -> x0, local copies, waits for them, and re-layouts: 3.16 us -> none
    pallas_call x1 -> x2, Pallas kernels: 25.1 us -> 25.5 us  [the longest x1 21.2 us: shards(): pl.pallas_call(make_first(rows, group), out_shape=[jax.ShapeDtypeStruct(s...]
where the time goes in v3:
time: 25.6 us; the launch traced here: 25.5 us
  Pallas kernels  25.5 us (100%)
    pallas_call x1, Pallas kernels, shards(): pl.pallas_call(make_first(rows, group), out_shape=[jax.ShapeDtypeStruct(s...  21.2 us
    pallas_call x1, Pallas kernels, shards(): pl.pallas_call(make_second(rows, group), out_shape=jax.ShapeDtypeStruct((...  4.24 us

profile of v3, /device:TPU:0, one launch (start us, length us, event | category | flops | bytes accessed | tf_op | source)
XLA Modules:
  0.0 25.5 jit_solution(1117869230644248752)
XLA Ops:
  0.0 21.2 %shard_map.64 = (f32[8704,128]{1,0:T(8,128)S(1)}, f32[2,64,16,8,128]{4,3,2,1,0:T(8,128)S(1)}, f32[2,16,8,128]{3,2,1,0:T(8,128)S(1)}, f32[256,128]{1,0:T(8,128)S(...) custom-call(bf16[512,2048]{1,0:T(8,128)(2,1)} %k_hbm.1, bf16[512,2048]{1,0:T(8,128)(2,1)} %v_hbm.1, f32[16,2048]{1,0:T(8,128)} %r_hbm.1, ...), custom_call_target="tpu_custom_call" | custom-call | tf_op jit(solution)/shard_map/pallas_call | solution.py:381
  21.2 4.2 %shard_map.65 = bf16[512,2048]{1,0:T(8,128)(2,1)} custom-call(bf16[512,2048]{1,0:T(8,128)(2,1)} %q_hbm.1, f32[8704,128]{1,0:T(8,128)S(1)} %get-tuple-element.11.xs, f32[2,64,16,8,128]{4,3,2,1,0:T(8,128)S(1)} %get-tuple-element.12.left, f32[2,16,8,128]{3,2,1,0:T(8,128)S(1)} %get-tuple-element.13.enter, f32[256,128]{1,0:T(8,128)S(1)} %get-tuple-element.14.fade, ...), custom_call_target="tpu_custom_call" | custom-call | tf_op jit(solution)/shard_map/pallas_call | solution.py:398

commit v4 on v0

v4 whole, which is shorter than its diff:
```python
import jax
import jax.numpy as jnp
from jax import lax
from jax.experimental import pallas as pl
from jax.experimental.pallas import tpu as pltpu
from jax.sharding import PartitionSpec as P

F32 = jnp.float32
LANES = 128
SUBS = 8
TILE = 16
BLOCK = 8
STEP = 32
ROWS = 512
SPAN = ROWS + STEP
CHUNKS = 4
SIDE = 4
MODES = 16
OWNED = MODES // SIDE
AWAY = (1, 3, 2, 0)
BACK = tuple(AWAY.index(-a % SIDE) for a in AWAY)
SELF = SIDE - 1
FIRST_VMEM = 36 << 20
SECOND_VMEM = 36 << 20


def reg(place, n):
    return pl.ds(pl.multiple_of((place * MODES + n) * SUBS, SUBS), SUBS)


def row(place, t):
    return pl.ds(pl.multiple_of((place * SPAN + t) * SUBS, SUBS), SUBS)


def tile(place, t, b):
    return pl.ds((place * SPAN + t) * SUBS + b, SUBS, stride=SUBS)


def first_kernel(
    q_hbm, k_hbm, v_hbm, r_hbm, d_hbm, g_hbm, xb, enter, fade, amp, qb,
    kb, vb, rb, db, gb, rate, raw, fade8, lead, taps, left, ends, heard, sums, earlier, before, starts,
    p_sem, k_sem, v_sem, q_sem, a_send, a_recv, b_send, b_recv, c_send, c_recv, t_send, t_recv,
):
    group = SUBS * LANES
    chunk = ROWS // CHUNKS
    half = lax.axis_index("half")
    ctx = lax.axis_index("ctx")
    z = ctx // SIDE
    y = lax.rem(ctx, SIDE)
    owner = (half, 1 - half)

    def columns(place):
        return pl.ds(pl.multiple_of(owner[place] * group, group), group)

    def load(hbm, buf, sem, place, c):
        at = pl.ds(c * chunk, chunk)
        return pltpu.make_async_copy(hbm.at[at, columns(place)], buf.at[place, at, :], sem.at[place, c])

    def remote(src, dst, send_sem, recv_sem, to_half, to_z, to_y):
        return pltpu.make_async_remote_copy(
            src_ref=src,
            dst_ref=dst,
            send_sem=send_sem,
            recv_sem=recv_sem,
            device_id={"half": to_half, "ctx": to_z * SIDE + to_y},
            device_id_type=pl.DeviceIdType.MESH,
        )

    def along(k):
        return lax.rem(y + AWAY[k], SIDE)

    def to_owner(k):
        return remote(
            ends.at[pl.ds(k * OWNED, OWNED)], heard.at[y], a_send.at[k], a_recv.at[k], half, z, along(k)
        )

    def to_later(dz):
        return remote(sums, earlier.at[z], b_send.at[dz - 1], b_recv.at[dz - 1], half, lax.rem(z + dz, SIDE), y)

    def to_same(k):
        return remote(
            starts.at[along(k)], enter.at[0, pl.ds(BACK[k] * OWNED, OWNED)], c_send.at[k], c_recv.at[k], half, z, along(k)
        )

    def to_twin(k):
        return remote(
            starts.at[along(k)], enter.at[1, pl.ds(BACK[k] * OWNED, OWNED)], t_send.at[k], t_recv.at[k], 1 - half, z, along(k)
        )

    barrier = pltpu.get_barrier_semaphore()

    def greet(to_half, to_z, to_y):
        pl.semaphore_signal(
            barrier,
            inc=1,
            device_id={"half": to_half, "ctx": to_z * SIDE + to_y},
            device_id_type=pl.DeviceIdType.MESH,
        )

    rates = [pltpu.make_async_copy(d_hbm.at[:, columns(p)], db.at[p], p_sem.at[p, 0]) for p in range(2)]
    others = [pltpu.make_async_copy(r_hbm.at[:, columns(p)], rb.at[p], p_sem.at[p, 1]) for p in range(2)]
    others += [
        pltpu.make_async_copy(
            g_hbm.at[pl.ds(pl.multiple_of(owner[p] * SUBS, SUBS), SUBS), :], gb.at[p], p_sem.at[p, 2]
        )
        for p in range(2)
    ]
    rates[0].start()
    for c in range(CHUNKS):
        load(k_hbm, kb, k_sem, 0, c).start()
        load(v_hbm, vb, v_sem, 0, c).start()
    for k in range(SIDE):
        if k != SELF:
            greet(half, z, along(k))
        greet(1 - half, z, along(k))
    for dz in range(1, SIDE):
        greet(half, lax.rem(z + dz, SIDE), y)
    rates[1].start()
    for copy in others:
        copy.start()
    for c in range(CHUNKS):
        load(k_hbm, kb, k_sem, 1, c).start()
        load(v_hbm, vb, v_sem, 1, c).start()
    for p in range(2):
        for c in range(CHUNKS):
            load(q_hbm, qb, q_sem, p, c).start()

    def turn(src, dst, place):
        for b in range(SUBS):
            lanes = pl.ds(b * LANES, LANES)
            for m in range(0, MODES, SUBS):
                at = pl.ds((place * MODES + m) * SUBS + b, SUBS, stride=SUBS)
                dst[at, :] = src[place, m : m + SUBS, lanes]

    modes = [along(k) * OWNED + e for k in range(SIDE) for e in range(OWNED)]

    def decays(place):
        for n, m in enumerate(modes):
            fade[reg(place, n), :] = jnp.exp(-rate[reg(place, m), :])

    rates[0].wait()
    turn(db, rate, 0)
    decays(0)
    for n, m in enumerate(modes):
        fade8[reg(0, n), :] = jnp.exp(-float(BLOCK) * rate[reg(0, m), :])

    def arrive(place, c):
        load(k_hbm, kb, k_sem, place, c).wait()
        load(v_hbm, vb, v_sem, place, c).wait()

    def spread(place, t, to):
        for b in range(SUBS):
            lanes = pl.ds(b * LANES, LANES)
            for i in range(0, STEP, TILE):
                at = pl.ds(t + i, TILE)
                x = kb[place, at, lanes].astype(F32) * vb[place, at, lanes].astype(F32)
                for j in range(0, TILE, SUBS):
                    xb[tile(place, to + i + j, b), :] = x[j : j + SUBS]

    def read(place, t):
        return [xb[row(place, t + j), :] for j in range(BLOCK)]

    def gather(slots, look, first, size, held):
        def body(i, held):
            t = pl.multiple_of(first + i * STEP, STEP)
            held = list(held)
            for s in range(0, STEP, BLOCK):
                xs = read(0, t + s)
                for at, n in enumerate(slots):
                    a = fade[reg(0, n), :]
                    e = xs[0]
                    for x in xs[1:]:
                        e = e * a + x
                    left[(t + s) // BLOCK, n] = e
                    held[at] = held[at] * fade8[reg(0, n), :] + e
            if look:
                spread(0, pl.multiple_of(jnp.minimum(t + STEP, first + size - STEP), STEP), t + STEP)
            return tuple(held)

        return lax.fori_loop(0, size // STEP, body, held)

    zeros = jnp.zeros((SUBS, LANES), F32)

    def leave(slots, held):
        for at, n in enumerate(slots):
            ends[n] = held[at]

    slots = range(2 * OWNED)
    held = (zeros,) * len(slots)
    for c in range(CHUNKS):
        arrive(0, c)
        spread(0, c * chunk, c * chunk)
        held = gather(slots, True, c * chunk, chunk, held)
    leave(slots, held)
    pl.semaphore_wait(barrier, 3 * SIDE - 2)
    to_owner(0).start()
    to_owner(1).start()
    for k in range(2, SIDE):
        slots = range(k * OWNED, (k + 1) * OWNED)
        leave(slots, gather(slots, False, 0, ROWS, (zeros,) * OWNED))
        if k != SELF:
            to_owner(k).start()
    for e in range(OWNED):
        heard[y, e] = ends[SELF * OWNED + e]

    rates[1].wait()
    turn(db, rate, 1)
    decays(1)
    for copy in others:
        copy.wait()
    for place in range(2):
        turn(rb, raw, place)
        for n, m in enumerate(modes):
            amp[reg(place, n), :] = raw[reg(place, m), :] * jnp.sqrt(rate[reg(place, m), :])
    terms = [amp[reg(0, n), :] for n in range(MODES)]
    for j in range(BLOCK):
        total = sum(terms[1:], terms[0])
        taps[reg(0, j), :] = total + gb[0] if j == 0 else total
        if j < BLOCK - 1:
            terms = [term * fade[reg(0, n), :] for n, term in enumerate(terms)]
        if j == 0:
            for n, term in enumerate(terms):
                lead[reg(0, n), :] = term

    def own(i, state):
        t = pl.multiple_of(i * STEP, STEP)
        state = list(state)
        for s in range(0, STEP, BLOCK):
            xs = read(0, t + s)
            ys = []
            for j in range(BLOCK):
                out = taps[reg(0, 0), :] * xs[j]
                for i in range(j):
                    out = out + taps[reg(0, j - i), :] * xs[i]
                ys.append(out)
            for n in range(MODES):
                a = fade[reg(0, n), :]
                now = state[n] * lead[reg(0, n), :]
                ys[0] = ys[0] + now
                for j in range(1, BLOCK):
                    now = now * a
                    ys[j] = ys[j] + now
                state[n] = state[n] * fade8[reg(0, n), :] + left[(t + s) // BLOCK, n]
            for j in range(BLOCK):
                xb[row(0, t + s + j), :] = ys[j]
        return tuple(state)

    def other(i, held):
        t = pl.multiple_of(i * STEP, STEP)
        held = list(held)
        g = gb[1]
        for s in range(0, STEP, BLOCK):
            xs = read(1, t + s)
            ys = [g * x for x in xs]
            for n in range(MODES):
                a = fade[reg(1, n), :]
                w = amp[reg(1, n), :]
                for j in range(BLOCK):
                    held[n] = held[n] * a + xs[j]
                    ys[j] = ys[j] + w * held[n]
            for j in range(BLOCK):
                xb[row(1, t + s + j), :] = ys[j]
        spread(1, pl.multiple_of(jnp.minimum(t + STEP, ROWS - STEP), STEP), t + STEP)
        return tuple(held)

    steps = ROWS // STEP
    late = jnp.where(y == 0, 2, jnp.where(y == 2, 0, 1))
    part_a = jnp.where(y == 0, steps, jnp.where(y == 2, 5, 11))
    part_b = jnp.where(z == 0, late // 2, jnp.where(z == SIDE - 1, 3 + 4 * late, 4 * late))

    state = lax.fori_loop(0, part_a, own, (zeros,) * MODES)

    for k in range(SIDE):
        if k != SELF:
            to_owner(k).wait()
    for e in range(OWNED):
        whole = jnp.exp(-float(ROWS) * rate[reg(0, y * OWNED + e), :])
        total = zeros
        for place in range(SIDE):
            before[place, e] = total
            total = total * whole + heard[place, e]
        sums[e] = total
    for dz in range(1, SIDE):

        @pl.when(z + dz < SIDE)
        def _(dz=dz):
            to_later(dz).start()

    lax.fori_loop(part_a, steps, own, state)
    for c in range(CHUNKS):
        arrive(1, c)
    spread(1, 0, 0)
    held = lax.fori_loop(0, part_b, other, (zeros,) * MODES)

    for dz in range(1, SIDE):

        @pl.when(z - dz >= 0)
        def _(dz=dz):
            to_later(dz).wait_recv()

    for e in range(OWNED):
        d = rate[reg(0, y * OWNED + e), :]
        row_long = jnp.exp(-float(SIDE * ROWS) * d)
        whole = jnp.exp(-float(ROWS) * d)
        total = lax.fori_loop(0, z, lambda i, total: total * row_long + earlier[i, e], zeros)
        for place in range(SIDE):
            starts[place, e] = total + before[place, e]
            total = total * whole
    for k in range(SIDE):
        if k != SELF:
            to_same(k).start()
        to_twin(k).start()
    for e in range(OWNED):
        enter[0, SELF * OWNED + e] = starts[y, e]

    lax.fori_loop(part_b, steps, other, held)

    for dz in range(1, SIDE):

        @pl.when(z + dz < SIDE)
        def _(dz=dz):
            to_later(dz).wait_send()

    for p in range(2):
        for c in range(CHUNKS):
            load(q_hbm, qb, q_sem, p, c).wait()
    for k in range(SIDE):
        if k != SELF:
            to_same(k).wait()
        to_twin(k).wait()


def second_kernel(xs, enter, fade, amp, qb, o_hbm, xb, ob, o_sem):
    group = SUBS * LANES
    chunk = ROWS // CHUNKS
    half = lax.axis_index("half")
    owner = (half, 1 - half)

    def store(place, c):
        at = pl.ds(c * chunk, chunk)
        columns = pl.ds(pl.multiple_of(owner[place] * group, group), group)
        return pltpu.make_async_copy(ob.at[place, at, :], o_hbm.at[at, columns], o_sem.at[place, c])

    for place in range(2):
        state = tuple(amp[reg(place, n), :] * enter[place, n] for n in range(MODES))
        for c in range(CHUNKS):

            def body(i, state, place=place, first=c * chunk):
                t = pl.multiple_of(first + i * TILE, TILE)
                state = list(state)
                for s in range(0, TILE, BLOCK):
                    ys = [xs[row(place, t + s + j), :] for j in range(BLOCK)]
                    for n in range(MODES):
                        a = fade[reg(place, n), :]
                        for j in range(BLOCK):
                            state[n] = state[n] * a
                            ys[j] = ys[j] + state[n]
                    for j in range(BLOCK):
                        xb[pl.ds((s + j) * SUBS, SUBS), :] = ys[j]
                for b in range(SUBS):
                    lanes = pl.ds(b * LANES, LANES)
                    out = jnp.concatenate([xb[pl.ds(j * SUBS + b, SUBS, stride=SUBS), :] for j in range(0, TILE, SUBS)])
                    gate = qb[place, pl.ds(t, TILE), lanes].astype(F32)
                    ob[place, pl.ds(t, TILE), lanes] = (gate * out).astype(jnp.bfloat16)
                return tuple(state)

            state = lax.fori_loop(0, chunk // TILE, body, state)
            store(place, c).start()
    for place in range(2):
        for c in range(CHUNKS):
            store(place, c).wait()


def shards(query_gate, key_gate, value_input, residues, decays, skip_gain):
    rows, width = key_gate.shape
    group = width // 2
    assert group == SUBS * LANES and rows == ROWS
    assert residues.shape[0] == MODES and lax.axis_size("ctx") == SIDE * SIDE
    wide = pltpu.VMEM((2, rows, group), jnp.bfloat16)
    table = (2 * MODES * SUBS, LANES)
    dma = pltpu.SemaphoreType.DMA
    hbm = pl.BlockSpec(memory_space=pltpu.HBM)
    vmem = pl.BlockSpec(memory_space=pltpu.VMEM)

    def registers(*shape):
        return pltpu.VMEM((*shape, SUBS, LANES), F32)

    operands = (query_gate, key_gate, value_input, residues, decays, skip_gain.reshape(2 * SUBS, LANES))
    kept = pl.pallas_call(
        first_kernel,
        out_shape=[
            jax.ShapeDtypeStruct((2 * SPAN * SUBS, LANES), F32),
            jax.ShapeDtypeStruct((2, MODES, SUBS, LANES), F32),
            jax.ShapeDtypeStruct(table, F32),
            jax.ShapeDtypeStruct(table, F32),
            jax.ShapeDtypeStruct((2, rows, group), jnp.bfloat16),
        ],
        in_specs=[hbm] * 6,
        out_specs=[vmem] * 5,
        scratch_shapes=[wide, wide]
        + [pltpu.VMEM((2, MODES, group), F32)] * 2
        + [registers(2)]
        + [pltpu.VMEM(table, F32)] * 5
        + [
            registers(rows // BLOCK, MODES),
            registers(MODES),
            registers(SIDE, OWNED),
            registers(OWNED),
            registers(SIDE, OWNED),
            registers(SIDE, OWNED),
            registers(SIDE, OWNED),
            dma((2, 3)),
        ]
        + [dma((2, CHUNKS))] * 3
        + [dma((SIDE,))] * 8,
        compiler_params=pltpu.CompilerParams(
            collective_id=0, has_side_effects=True, vmem_limit_bytes=FIRST_VMEM
        ),
    )(*(pltpu.with_memory_space_constraint(x, pltpu.HBM) for x in operands))
    return pl.pallas_call(
        second_kernel,
        out_shape=jax.ShapeDtypeStruct((rows, width), jnp.bfloat16),
        in_specs=[vmem] * 5,
        out_specs=hbm,
        scratch_shapes=[pltpu.VMEM((TILE * SUBS, LANES), F32), wide, dma((2, CHUNKS))],
        compiler_params=pltpu.CompilerParams(vmem_limit_bytes=SECOND_VMEM),
    )(*kept)


def solution(mesh):
    placed = (
        P("ctx", "chan"),
        P("ctx", "chan"),
        P("ctx", "chan"),
        P(None, "chan"),
        P(None, "chan"),
        P("chan"),
    )
    return jax.shard_map(shards, mesh=mesh, in_specs=placed, out_specs=P("ctx", "chan"), check_vma=False)
```

time: 723 us -> 23.2 us (0.03); the launches traced: 711 us -> 23.1 us
  waiting for transfers between devices: 417 us -> 0 us
  other arithmetic: 98.7 us -> 0 us
  matrix products: 77 us -> 0 us
  blocking collectives: 51 us -> 0 us
  local copies, waits for them, and re-layouts: 32.7 us -> 0 us
  Pallas kernels: 0 us -> 23.1 us
  starting transfers between devices: 20.3 us -> 0 us
  between operations: 14.1 us -> 0.01 us
    all_to_all x3 -> x0, waiting for transfers between devices: 303 us -> none  [the longest x2 242 us: spread_positions(): lax.all_to_all(field, 'ctx', split_axis=1, concat_axis=1, tiled=True)]
    psum x1 -> x0, waiting for transfers between devices: 114 us -> none  [shards(): full_conv = lax.psum(half_term, 'half')]
    dot_general x4 -> x0, matrix products: 77 us -> none  [apply_table(): jnp.dot(matrix, flat_data, precision=lax.Precision.HIGHEST, preferred_ele...]
    all_to_all x1 -> x0, blocking collectives: 51 us -> none  [spread_positions(): lax.all_to_all(half_term, 'ctx', split_axis=0, concat_axis=1, tiled=True)]
    reduce_sum x8 -> x0, other arithmetic: 31.6 us -> none  [one_block(): return (jnp.sum(factor * real_den, 0), -jnp.sum(factor * imag_den, 0))]
    pallas_call x0 -> x2, Pallas kernels: none -> 23.1 us  [the longest x1 16.8 us: shards(): pl.pallas_call(first_kernel, out_shape=[jax.ShapeDtypeStruct((2 * SPAN *...]
    all_to_all x3 -> x0, starting transfers between devices: 20.1 us -> none  [the longest x2 13.3 us: spread_positions(): lax.all_to_all(field, 'ctx', split_axis=1, concat_axis=1, tiled=True)]
    unnamed x20 -> x0, local copies, waits for them, and re-layouts: 19.6 us -> none
  transfers between devices with their start and end apart: 4 -> 0, of which waited for: 4 -> 0; matrix products, arithmetic and copies ran while one was open for 8% -> 0% of each run, Pallas kernels for 0% -> 0%
where the time goes in v4:
time: 23.2 us; the launch traced here: 23.1 us
  Pallas kernels  23.1 us (100%)
    pallas_call x1, Pallas kernels, shards(): pl.pallas_call(first_kernel, out_shape=[jax.ShapeDtypeStruct((2 * SPAN *...  16.8 us
    pallas_call x1, Pallas kernels, shards(): pl.pallas_call(second_kernel, out_shape=jax.ShapeDtypeStruct((rows, width...  6.34 us

profile of v4, /device:TPU:96, one launch (start us, length us, event | category | flops | bytes accessed | tf_op | source)
XLA Modules:
  0.0 23.1 jit_solution(11065260070791573607)
XLA Ops:
  0.0 16.8 %shard_map.64 = (f32[8704,128]{1,0:T(8,128)S(1)}, f32[2,16,8,128]{3,2,1,0:T(8,128)S(1)}, f32[256,128]{1,0:T(8,128)S(1)}, f32[256,128]{1,0:T(8,128)S(1)}, bf16[2,512,1024]{2,1,0:T(8,128)(2,1)S(1)}) custom-call(bf16[512,2048]{1,0:T(8,128)(2,1)} %q_hbm.1, bf16[512,2048]{1,0:T(8,128)(2,1)} %k_hbm.1, bf16[512,2048]{1,0:T(8,128)(2,1)} %v_hbm.1, f32[16,2048]{1,0:T(8,128)} %r_hbm.1, ...), custom_call_target="tpu_custom_call" | custom-call | tf_op jit(solution)/shard_map/pallas_call | solution.py:389
  16.8 6.3 %shard_map.65 = bf16[512,2048]{1,0:T(8,128)(2,1)} custom-call(f32[8704,128]{1,0:T(8,128)S(1)} %get-tuple-element.10.xs, f32[2,16,8,128]{3,2,1,0:T(8,128)S(1)} %get-tuple-element.11.enter, f32[256,128]{1,0:T(8,128)S(1)} %get-tuple-element.12.fade, f32[256,128]{1,0:T(8,128)S(1)} %get-tuple-element.13.amp, bf16[2,512,1024]{2,1,0:T(8,128)(2,1)S(1)} %get-tuple-element.14.qb), custom_call_target="tpu_custom_call" | custom-call | tf_op jit(solution)/shard_map/pallas_call | solution.py:420

commit v5 on v4

--- a/solution.py
+++ b/solution.py
@@ -17,7 +17,7 @@
 SIDE = 4
 MODES = 16
 OWNED = MODES // SIDE
-AWAY = (1, 3, 2, 0)
+AWAY = (2, 1, 3, 0)
 BACK = tuple(AWAY.index(-a % SIDE) for a in AWAY)
 SELF = SIDE - 1
 FIRST_VMEM = 36 << 20
@@ -222,28 +222,16 @@
             for n, term in enumerate(terms):
                 lead[reg(0, n), :] = term
 
-    def own(i, state):
+    def own(i, carry):
         t = pl.multiple_of(i * STEP, STEP)
-        state = list(state)
         for s in range(0, STEP, BLOCK):
             xs = read(0, t + s)
-            ys = []
             for j in range(BLOCK):
                 out = taps[reg(0, 0), :] * xs[j]
                 for i in range(j):
                     out = out + taps[reg(0, j - i), :] * xs[i]
-                ys.append(out)
-            for n in range(MODES):
-                a = fade[reg(0, n), :]
-                now = state[n] * lead[reg(0, n), :]
-                ys[0] = ys[0] + now
-                for j in range(1, BLOCK):
-                    now = now * a
-                    ys[j] = ys[j] + now
-                state[n] = state[n] * fade8[reg(0, n), :] + left[(t + s) // BLOCK, n]
-            for j in range(BLOCK):
-                xb[row(0, t + s + j), :] = ys[j]
-        return tuple(state)
+                xb[row(0, t + s + j), :] = out
+        return carry
 
     def other(i, held):
         t = pl.multiple_of(i * STEP, STEP)
@@ -264,11 +252,18 @@
         return tuple(held)
 
     steps = ROWS // STEP
-    late = jnp.where(y == 0, 2, jnp.where(y == 2, 0, 1))
-    part_a = jnp.where(y == 0, steps, jnp.where(y == 2, 5, 11))
-    part_b = jnp.where(z == 0, late // 2, jnp.where(z == SIDE - 1, 3 + 4 * late, 4 * late))
-
-    state = lax.fori_loop(0, part_a, own, (zeros,) * MODES)
+
+    def by_place(*choices):
+        return jnp.where(y < 2, jnp.where(y == 0, choices[0], choices[1]), jnp.where(y == 2, choices[2], choices[3]))
+
+    part_a = by_place(7, 4, 0, 1)
+    part_b = jnp.where(z == 0, part_a, jnp.where(z == SIDE - 1, by_place(16, 13, 9, 10), by_place(11, 8, 4, 6)))
+
+    lax.fori_loop(0, steps, own, 0)
+    for c in range(CHUNKS):
+        arrive(1, c)
+    spread(1, 0, 0)
+    held = lax.fori_loop(0, part_a, other, (zeros,) * MODES)
 
     for k in range(SIDE):
         if k != SELF:
@@ -286,11 +281,7 @@
         def _(dz=dz):
             to_later(dz).start()
 
-    lax.fori_loop(part_a, steps, own, state)
-    for c in range(CHUNKS):
-        arrive(1, c)
-    spread(1, 0, 0)
-    held = lax.fori_loop(0, part_b, other, (zeros,) * MODES)
+    held = lax.fori_loop(part_a, part_b, other, held)
 
     for dz in range(1, SIDE):
 
@@ -321,16 +312,42 @@
         def _(dz=dz):
             to_later(dz).wait_send()
 
+    def pour(blocks):
+        slots = [k * OWNED + e for k in blocks for e in range(OWNED)]
+
+        def body(i, state):
+            t = pl.multiple_of(i * STEP, STEP)
+            state = list(state)
+            for s in range(0, STEP, BLOCK):
+                ys = read(0, t + s)
+                for at, n in enumerate(slots):
+                    a = fade[reg(0, n), :]
+                    now = state[at] * lead[reg(0, n), :]
+                    ys[0] = ys[0] + now
+                    for j in range(1, BLOCK):
+                        now = now * a
+                        ys[j] = ys[j] + now
+                    state[at] = state[at] * fade8[reg(0, n), :] + left[(t + s) // BLOCK, n]
+                for j in range(BLOCK):
+                    xb[row(0, t + s + j), :] = ys[j]
+            return tuple(state)
+
+        lax.fori_loop(0, steps, body, tuple(enter[0, n] for n in slots))
+
+    pour((SELF,))
+    to_same(BACK[1]).wait()
+    to_same(BACK[2]).wait()
+    pour((1, 2))
+    to_same(BACK[0]).wait()
+    pour((0,))
     for p in range(2):
         for c in range(CHUNKS):
             load(q_hbm, qb, q_sem, p, c).wait()
     for k in range(SIDE):
-        if k != SELF:
-            to_same(k).wait()
         to_twin(k).wait()
 
 
-def second_kernel(xs, enter, fade, amp, qb, o_hbm, xb, ob, o_sem):
+def second_kernel(xs, enter, fade, amp, qb, o_hbm, xb, state, ob, o_sem):
     group = SUBS * LANES
     chunk = ROWS // CHUNKS
     half = lax.axis_index("half")
@@ -341,31 +358,43 @@
         columns = pl.ds(pl.multiple_of(owner[place] * group, group), group)
         return pltpu.make_async_copy(ob.at[place, at, :], o_hbm.at[at, columns], o_sem.at[place, c])
 
-    for place in range(2):
-        state = tuple(amp[reg(place, n), :] * enter[place, n] for n in range(MODES))
-        for c in range(CHUNKS):
-
-            def body(i, state, place=place, first=c * chunk):
-                t = pl.multiple_of(first + i * TILE, TILE)
-                state = list(state)
-                for s in range(0, TILE, BLOCK):
-                    ys = [xs[row(place, t + s + j), :] for j in range(BLOCK)]
-                    for n in range(MODES):
-                        a = fade[reg(place, n), :]
-                        for j in range(BLOCK):
-                            state[n] = state[n] * a
-                            ys[j] = ys[j] + state[n]
+    def gate(place, t, turned):
+        for b in range(SUBS):
+            lanes = pl.ds(b * LANES, LANES)
+            out = jnp.concatenate([turned(j, b) for j in range(0, TILE, SUBS)])
+            ob[place, pl.ds(t, TILE), lanes] = (qb[place, pl.ds(t, TILE), lanes].astype(F32) * out).astype(jnp.bfloat16)
+
+    for c in range(CHUNKS):
+
+        def plain(i, carry, first=c * chunk):
+            t = pl.multiple_of(first + i * TILE, TILE)
+            gate(0, t, lambda j, b: xs[tile(0, t + j, b), :])
+            return carry
+
+        lax.fori_loop(0, chunk // TILE, plain, 0)
+        store(0, c).start()
+    for n in range(MODES):
+        state[n] = amp[reg(1, n), :] * enter[1, n]
+    for c in range(CHUNKS):
+
+        def body(i, carry, first=c * chunk):
+            t = pl.multiple_of(first + i * TILE, TILE)
+            for s in range(0, TILE, BLOCK):
+                ys = [xs[row(1, t + s + j), :] for j in range(BLOCK)]
+                for n in range(MODES):
+                    a = fade[reg(1, n), :]
+                    now = state[n]
                     for j in range(BLOCK):
-                        xb[pl.ds((s + j) * SUBS, SUBS), :] = ys[j]
-                for b in range(SUBS):
-                    lanes = pl.ds(b * LANES, LANES)
-                    out = jnp.concatenate([xb[pl.ds(j * SUBS + b, SUBS, stride=SUBS), :] for j in range(0, TILE, SUBS)])
-                    gate = qb[place, pl.ds(t, TILE), lanes].astype(F32)
-                    ob[place, pl.ds(t, TILE), lanes] = (gate * out).astype(jnp.bfloat16)
-                return tuple(state)
-
-            state = lax.fori_loop(0, chunk // TILE, body, state)
-            store(place, c).start()
+                        now = now * a
+                        ys[j] = ys[j] + now
+                    state[n] = now
+                for j in range(BLOCK):
+                    xb[pl.ds((s + j) * SUBS, SUBS), :] = ys[j]
+            gate(1, t, lambda j, b: xb[pl.ds(j * SUBS + b, SUBS, stride=SUBS), :])
+            return carry
+
+        lax.fori_loop(0, chunk // TILE, body, 0)
+        store(1, c).start()
     for place in range(2):
         for c in range(CHUNKS):
             store(place, c).wait()
@@ -422,7 +451,7 @@
         out_shape=jax.ShapeDtypeStruct((rows, width), jnp.bfloat16),
         in_specs=[vmem] * 5,
         out_specs=hbm,
-        scratch_shapes=[pltpu.VMEM((TILE * SUBS, LANES), F32), wide, dma((2, CHUNKS))],
+        scratch_shapes=[pltpu.VMEM((TILE * SUBS, LANES), F32), registers(MODES), wide, dma((2, CHUNKS))],
         compiler_params=pltpu.CompilerParams(vmem_limit_bytes=SECOND_VMEM),
     )(*kept)
 

time: 23.2 us -> 21.4 us (0.922)
  Pallas kernels: 23.1 us -> 21.3 us
    pallas_call x1, Pallas kernels: 6.34 us -> 4.11 us  [shards(): pl.pallas_call(second_kernel, out_shape=jax.ShapeDtypeStruct((rows, width...]
    pallas_call x1, Pallas kernels: 16.8 us -> 17.2 us  [shards(): pl.pallas_call(first_kernel, out_shape=[jax.ShapeDtypeStruct((2 * SPAN *...]
where the time goes in v5:
time: 21.4 us; the launch traced here: 21.3 us
  Pallas kernels  21.3 us (100%)
    pallas_call x1, Pallas kernels, shards(): pl.pallas_call(first_kernel, out_shape=[jax.ShapeDtypeStruct((2 * SPAN *...  17.2 us
    pallas_call x1, Pallas kernels, shards(): pl.pallas_call(second_kernel, out_shape=jax.ShapeDtypeStruct((rows, width...  4.11 us

profile of v5, /device:TPU:96, one launch (start us, length us, event | category | flops | bytes accessed | tf_op | source)
XLA Modules:
  0.0 21.3 jit_solution(13345672436377707551)
XLA Ops:
  0.0 17.2 %shard_map.64 = (f32[8704,128]{1,0:T(8,128)S(1)}, f32[2,16,8,128]{3,2,1,0:T(8,128)S(1)}, f32[256,128]{1,0:T(8,128)S(1)}, f32[256,128]{1,0:T(8,128)S(1)}, bf16[2,512,1024]{2,1,0:T(8,128)(2,1)S(1)}) custom-call(bf16[512,2048]{1,0:T(8,128)(2,1)} %q_hbm.1, bf16[512,2048]{1,0:T(8,128)(2,1)} %k_hbm.1, bf16[512,2048]{1,0:T(8,128)(2,1)} %v_hbm.1, f32[16,2048]{1,0:T(8,128)} %r_hbm.1, ...), custom_call_target="tpu_custom_call" | custom-call | tf_op jit(solution)/shard_map/pallas_call | solution.py:418
  17.2 4.1 %shard_map.65 = bf16[512,2048]{1,0:T(8,128)(2,1)} custom-call(f32[8704,128]{1,0:T(8,128)S(1)} %get-tuple-element.10.xs, f32[2,16,8,128]{3,2,1,0:T(8,128)S(1)} %get-tuple-element.11.enter, f32[256,128]{1,0:T(8,128)S(1)} %get-tuple-element.12.fade, f32[256,128]{1,0:T(8,128)S(1)} %get-tuple-element.13.amp, bf16[2,512,1024]{2,1,0:T(8,128)(2,1)S(1)} %get-tuple-element.14.qb), custom_call_target="tpu_custom_call" | custom-call | tf_op jit(solution)/shard_map/pallas_call | solution.py:449

commit v6 on v5

--- a/solution.py
+++ b/solution.py
@@ -256,8 +256,8 @@
     def by_place(*choices):
         return jnp.where(y < 2, jnp.where(y == 0, choices[0], choices[1]), jnp.where(y == 2, choices[2], choices[3]))
 
-    part_a = by_place(7, 4, 0, 1)
-    part_b = jnp.where(z == 0, part_a, jnp.where(z == SIDE - 1, by_place(16, 13, 9, 10), by_place(11, 8, 4, 6)))
+    part_a = by_place(7, 4, 4, 2)
+    part_b = jnp.where(z == 0, part_a, jnp.where(z == SIDE - 1, by_place(16, 12, 12, 11), by_place(11, 8, 9, 7)))
 
     lax.fori_loop(0, steps, own, 0)
     for c in range(CHUNKS):
@@ -364,22 +364,13 @@
             out = jnp.concatenate([turned(j, b) for j in range(0, TILE, SUBS)])
             ob[place, pl.ds(t, TILE), lanes] = (qb[place, pl.ds(t, TILE), lanes].astype(F32) * out).astype(jnp.bfloat16)
 
-    for c in range(CHUNKS):
-
-        def plain(i, carry, first=c * chunk):
-            t = pl.multiple_of(first + i * TILE, TILE)
-            gate(0, t, lambda j, b: xs[tile(0, t + j, b), :])
-            return carry
-
-        lax.fori_loop(0, chunk // TILE, plain, 0)
-        store(0, c).start()
     for n in range(MODES):
         state[n] = amp[reg(1, n), :] * enter[1, n]
     for c in range(CHUNKS):
 
         def body(i, carry, first=c * chunk):
-            t = pl.multiple_of(first + i * TILE, TILE)
-            for s in range(0, TILE, BLOCK):
+            t = pl.multiple_of(first + i * STEP, STEP)
+            for s in range(0, STEP, BLOCK):
                 ys = [xs[row(1, t + s + j), :] for j in range(BLOCK)]
                 for n in range(MODES):
                     a = fade[reg(1, n), :]
@@ -390,10 +381,14 @@
                     state[n] = now
                 for j in range(BLOCK):
                     xb[pl.ds((s + j) * SUBS, SUBS), :] = ys[j]
-            gate(1, t, lambda j, b: xb[pl.ds(j * SUBS + b, SUBS, stride=SUBS), :])
+                if (s + BLOCK) % TILE == 0:
+                    at = s + BLOCK - TILE
+                    gate(0, t + at, lambda j, b, at=at: xs[tile(0, t + at + j, b), :])
+                    gate(1, t + at, lambda j, b, at=at: xb[pl.ds((at + j) * SUBS + b, SUBS, stride=SUBS), :])
             return carry
 
-        lax.fori_loop(0, chunk // TILE, body, 0)
+        lax.fori_loop(0, chunk // STEP, body, 0)
+        store(0, c).start()
         store(1, c).start()
     for place in range(2):
         for c in range(CHUNKS):
@@ -451,7 +446,7 @@
         out_shape=jax.ShapeDtypeStruct((rows, width), jnp.bfloat16),
         in_specs=[vmem] * 5,
         out_specs=hbm,
-        scratch_shapes=[pltpu.VMEM((TILE * SUBS, LANES), F32), registers(MODES), wide, dma((2, CHUNKS))],
+        scratch_shapes=[pltpu.VMEM((STEP * SUBS, LANES), F32), registers(MODES), wide, dma((2, CHUNKS))],
         compiler_params=pltpu.CompilerParams(vmem_limit_bytes=SECOND_VMEM),
     )(*kept)
 

time: 21.4 us -> 21.1 us (0.986)
  Pallas kernels: 21.3 us -> 21 us
    pallas_call x1, Pallas kernels: 4.11 us -> 3.78 us  [shards(): pl.pallas_call(second_kernel, out_shape=jax.ShapeDtypeStruct((rows, width...]
where the time goes in v6:
time: 21.1 us; the launch traced here: 21 us
  Pallas kernels  21 us (100%)
    pallas_call x1, Pallas kernels, shards(): pl.pallas_call(first_kernel, out_shape=[jax.ShapeDtypeStruct((2 * SPAN *...  17.2 us
    pallas_call x1, Pallas kernels, shards(): pl.pallas_call(second_kernel, out_shape=jax.ShapeDtypeStruct((rows, width...  3.78 us

profile of v6, /device:TPU:96, one launch (start us, length us, event | category | flops | bytes accessed | tf_op | source)
XLA Modules:
  0.0 21.0 jit_solution(9993807576934590666)
XLA Ops:
  0.0 17.2 %shard_map.64 = (f32[8704,128]{1,0:T(8,128)S(1)}, f32[2,16,8,128]{3,2,1,0:T(8,128)S(1)}, f32[256,128]{1,0:T(8,128)S(1)}, f32[256,128]{1,0:T(8,128)S(1)}, bf16[2,512,1024]{2,1,0:T(8,128)(2,1)S(1)}) custom-call(bf16[512,2048]{1,0:T(8,128)(2,1)} %q_hbm.1, bf16[512,2048]{1,0:T(8,128)(2,1)} %k_hbm.1, bf16[512,2048]{1,0:T(8,128)(2,1)} %v_hbm.1, f32[16,2048]{1,0:T(8,128)} %r_hbm.1, ...), custom_call_target="tpu_custom_call" | custom-call | tf_op jit(solution)/shard_map/pallas_call | solution.py:413
  17.2 3.8 %shard_map.65 = bf16[512,2048]{1,0:T(8,128)(2,1)} custom-call(f32[8704,128]{1,0:T(8,128)S(1)} %get-tuple-element.10.xs, f32[2,16,8,128]{3,2,1,0:T(8,128)S(1)} %get-tuple-element.11.enter, f32[256,128]{1,0:T(8,128)S(1)} %get-tuple-element.12.fade, f32[256,128]{1,0:T(8,128)S(1)} %get-tuple-element.13.amp, bf16[2,512,1024]{2,1,0:T(8,128)(2,1)S(1)} %get-tuple-element.14.qb), custom_call_target="tpu_custom_call" | custom-call | tf_op jit(solution)/shard_map/pallas_call | solution.py:444

commit v7 on v6

--- a/solution.py
+++ b/solution.py
@@ -257,7 +257,7 @@
         return jnp.where(y < 2, jnp.where(y == 0, choices[0], choices[1]), jnp.where(y == 2, choices[2], choices[3]))
 
     part_a = by_place(7, 4, 4, 2)
-    part_b = jnp.where(z == 0, part_a, jnp.where(z == SIDE - 1, by_place(16, 12, 12, 11), by_place(11, 8, 9, 7)))
+    part_b = jnp.where(z == 0, part_a, jnp.where(z == SIDE - 1, by_place(13, 10, 9, 8), by_place(11, 8, 9, 7)))
 
     lax.fori_loop(0, steps, own, 0)
     for c in range(CHUNKS):
@@ -335,11 +335,9 @@
         lax.fori_loop(0, steps, body, tuple(enter[0, n] for n in slots))
 
     pour((SELF,))
-    to_same(BACK[1]).wait()
-    to_same(BACK[2]).wait()
-    pour((1, 2))
-    to_same(BACK[0]).wait()
-    pour((0,))
+    for k in (2, 1, 0):
+        to_same(BACK[k]).wait()
+        pour((k,))
     for p in range(2):
         for c in range(CHUNKS):
             load(q_hbm, qb, q_sem, p, c).wait()

time: 21.1 us -> 20.6 us (0.976)
  Pallas kernels: 21 us -> 20.5 us
    pallas_call x1, Pallas kernels: 17.2 us -> 16.7 us  [shards(): pl.pallas_call(first_kernel, out_shape=[jax.ShapeDtypeStruct((2 * SPAN *...]
where the time goes in v7:
time: 20.6 us; the launch traced here: 20.5 us
  Pallas kernels  20.5 us (100%)
    pallas_call x1, Pallas kernels, shards(): pl.pallas_call(first_kernel, out_shape=[jax.ShapeDtypeStruct((2 * SPAN *...  16.7 us
    pallas_call x1, Pallas kernels, shards(): pl.pallas_call(second_kernel, out_shape=jax.ShapeDtypeStruct((rows, width...  3.78 us

profile of v7, /device:TPU:96, one launch (start us, length us, event | category | flops | bytes accessed | tf_op | source)
XLA Modules:
  0.0 20.5 jit_solution(7558260244787188986)
XLA Ops:
  0.0 16.7 %shard_map.64 = (f32[8704,128]{1,0:T(8,128)S(1)}, f32[2,16,8,128]{3,2,1,0:T(8,128)S(1)}, f32[256,128]{1,0:T(8,128)S(1)}, f32[256,128]{1,0:T(8,128)S(1)}, bf16[2,512,1024]{2,1,0:T(8,128)(2,1)S(1)}) custom-call(bf16[512,2048]{1,0:T(8,128)(2,1)} %q_hbm.1, bf16[512,2048]{1,0:T(8,128)(2,1)} %k_hbm.1, bf16[512,2048]{1,0:T(8,128)(2,1)} %v_hbm.1, f32[16,2048]{1,0:T(8,128)} %r_hbm.1, ...), custom_call_target="tpu_custom_call" | custom-call | tf_op jit(solution)/shard_map/pallas_call | solution.py:411
  16.7 3.8 %shard_map.65 = bf16[512,2048]{1,0:T(8,128)(2,1)} custom-call(f32[8704,128]{1,0:T(8,128)S(1)} %get-tuple-element.10.xs, f32[2,16,8,128]{3,2,1,0:T(8,128)S(1)} %get-tuple-element.11.enter, f32[256,128]{1,0:T(8,128)S(1)} %get-tuple-element.12.fade, f32[256,128]{1,0:T(8,128)S(1)} %get-tuple-element.13.amp, bf16[2,512,1024]{2,1,0:T(8,128)(2,1)S(1)} %get-tuple-element.14.qb), custom_call_target="tpu_custom_call" | custom-call | tf_op jit(solution)/shard_map/pallas_call | solution.py:442

commit v8 on v7

--- a/solution.py
+++ b/solution.py
@@ -11,9 +11,11 @@
 TILE = 16
 BLOCK = 8
 STEP = 32
+WIDE = 64
 ROWS = 512
 SPAN = ROWS + STEP
 CHUNKS = 4
+PARTS = 8
 SIDE = 4
 MODES = 16
 OWNED = MODES // SIDE
@@ -161,10 +163,12 @@
         return [xb[row(place, t + j), :] for j in range(BLOCK)]
 
     def gather(slots, look, first, size, held):
+        step = STEP if look else WIDE
+
         def body(i, held):
-            t = pl.multiple_of(first + i * STEP, STEP)
+            t = pl.multiple_of(first + i * step, step)
             held = list(held)
-            for s in range(0, STEP, BLOCK):
+            for s in range(0, step, BLOCK):
                 xs = read(0, t + s)
                 for at, n in enumerate(slots):
                     a = fade[reg(0, n), :]
@@ -177,7 +181,7 @@
                 spread(0, pl.multiple_of(jnp.minimum(t + STEP, first + size - STEP), STEP), t + STEP)
             return tuple(held)
 
-        return lax.fori_loop(0, size // STEP, body, held)
+        return lax.fori_loop(0, size // step, body, held)
 
     zeros = jnp.zeros((SUBS, LANES), F32)
 
@@ -192,14 +196,30 @@
         spread(0, c * chunk, c * chunk)
         held = gather(slots, True, c * chunk, chunk, held)
     leave(slots, held)
-    pl.semaphore_wait(barrier, 3 * SIDE - 2)
-    to_owner(0).start()
-    to_owner(1).start()
+    far = (y > 0) & (z > 0)
+
+    @pl.when(far)
+    def _():
+        pl.semaphore_wait(barrier, 3 * SIDE - 2)
+        to_owner(0).start()
+        to_owner(1).start()
+
     for k in range(2, SIDE):
         slots = range(k * OWNED, (k + 1) * OWNED)
         leave(slots, gather(slots, False, 0, ROWS, (zeros,) * OWNED))
         if k != SELF:
-            to_owner(k).start()
+
+            @pl.when(far)
+            def _(k=k):
+                to_owner(k).start()
+
+            @pl.when(~far)
+            def _():
+                pl.semaphore_wait(barrier, 3 * SIDE - 2)
+                to_owner(0).start()
+                to_owner(1).start()
+                to_owner(2).start()
+
     for e in range(OWNED):
         heard[y, e] = ends[SELF * OWNED + e]
 
@@ -316,9 +336,9 @@
         slots = [k * OWNED + e for k in blocks for e in range(OWNED)]
 
         def body(i, state):
-            t = pl.multiple_of(i * STEP, STEP)
+            t = pl.multiple_of(i * WIDE, WIDE)
             state = list(state)
-            for s in range(0, STEP, BLOCK):
+            for s in range(0, WIDE, BLOCK):
                 ys = read(0, t + s)
                 for at, n in enumerate(slots):
                     a = fade[reg(0, n), :]
@@ -332,22 +352,26 @@
                     xb[row(0, t + s + j), :] = ys[j]
             return tuple(state)
 
-        lax.fori_loop(0, steps, body, tuple(enter[0, n] for n in slots))
+        lax.fori_loop(0, ROWS // WIDE, body, tuple(enter[0, n] for n in slots))
 
     pour((SELF,))
-    for k in (2, 1, 0):
-        to_same(BACK[k]).wait()
-        pour((k,))
     for p in range(2):
         for c in range(CHUNKS):
             load(q_hbm, qb, q_sem, p, c).wait()
     for k in range(SIDE):
-        to_twin(k).wait()
+        if k != SELF:
+            to_same(k).wait_send()
+        to_twin(k).wait_send()
+    for k in (2, 1, 0):
+        to_same(BACK[k]).wait_recv()
+        pour((k,))
+    for k in range(SIDE):
+        to_twin(k).wait_recv()
 
 
 def second_kernel(xs, enter, fade, amp, qb, o_hbm, xb, state, ob, o_sem):
     group = SUBS * LANES
-    chunk = ROWS // CHUNKS
+    chunk = ROWS // PARTS
     half = lax.axis_index("half")
     owner = (half, 1 - half)
 
@@ -364,7 +388,7 @@
 
     for n in range(MODES):
         state[n] = amp[reg(1, n), :] * enter[1, n]
-    for c in range(CHUNKS):
+    for c in range(PARTS):
 
         def body(i, carry, first=c * chunk):
             t = pl.multiple_of(first + i * STEP, STEP)
@@ -389,7 +413,7 @@
         store(0, c).start()
         store(1, c).start()
     for place in range(2):
-        for c in range(CHUNKS):
+        for c in range(PARTS):
             store(place, c).wait()
 
 
@@ -444,7 +468,7 @@
         out_shape=jax.ShapeDtypeStruct((rows, width), jnp.bfloat16),
         in_specs=[vmem] * 5,
         out_specs=hbm,
-        scratch_shapes=[pltpu.VMEM((STEP * SUBS, LANES), F32), registers(MODES), wide, dma((2, CHUNKS))],
+        scratch_shapes=[pltpu.VMEM((STEP * SUBS, LANES), F32), registers(MODES), wide, dma((2, PARTS))],
         compiler_params=pltpu.CompilerParams(vmem_limit_bytes=SECOND_VMEM),
     )(*kept)
 

time: 20.6 us -> 20.2 us (0.981)
  the two profiles are of different devices: /device:TPU:96 before, /device:TPU:34 now
where the time goes in v8:
time: 20.2 us; the launch traced here: 20.1 us
  Pallas kernels  20.1 us (100%)
    pallas_call x1, Pallas kernels, shards(): pl.pallas_call(first_kernel, out_shape=[jax.ShapeDtypeStruct((2 * SPAN *...  16.3 us
    pallas_call x1, Pallas kernels, shards(): pl.pallas_call(second_kernel, out_shape=jax.ShapeDtypeStruct((rows, width...  3.76 us

profile of v8, /device:TPU:34, one launch (start us, length us, event | category | flops | bytes accessed | tf_op | source)
XLA Modules:
  0.0 20.1 jit_solution(12982584390629372439)
XLA Ops:
  0.0 16.3 %shard_map.64 = (f32[8704,128]{1,0:T(8,128)S(1)}, f32[2,16,8,128]{3,2,1,0:T(8,128)S(1)}, f32[256,128]{1,0:T(8,128)S(1)}, f32[256,128]{1,0:T(8,128)S(1)}, bf16[2,512,1024]{2,1,0:T(8,128)(2,1)S(1)}) custom-call(bf16[512,2048]{1,0:T(8,128)(2,1)} %q_hbm.1, bf16[512,2048]{1,0:T(8,128)(2,1)} %k_hbm.1, bf16[512,2048]{1,0:T(8,128)(2,1)} %v_hbm.1, f32[16,2048]{1,0:T(8,128)} %r_hbm.1, ...), custom_call_target="tpu_custom_call" | custom-call | tf_op jit(solution)/shard_map/pallas_call | solution.py:435
  16.3 3.8 %shard_map.65 = bf16[512,2048]{1,0:T(8,128)(2,1)} custom-call(f32[8704,128]{1,0:T(8,128)S(1)} %get-tuple-element.10.xs, f32[2,16,8,128]{3,2,1,0:T(8,128)S(1)} %get-tuple-element.11.enter, f32[256,128]{1,0:T(8,128)S(1)} %get-tuple-element.12.fade, f32[256,128]{1,0:T(8,128)S(1)} %get-tuple-element.13.amp, bf16[2,512,1024]{2,1,0:T(8,128)(2,1)S(1)} %get-tuple-element.14.qb), custom_call_target="tpu_custom_call" | custom-call | tf_op jit(solution)/shard_map/pallas_call | solution.py:466

commit v9 on v8

--- a/solution.py
+++ b/solution.py
@@ -391,8 +391,8 @@
     for c in range(PARTS):
 
         def body(i, carry, first=c * chunk):
-            t = pl.multiple_of(first + i * STEP, STEP)
-            for s in range(0, STEP, BLOCK):
+            t = pl.multiple_of(first + i * WIDE, WIDE)
+            for s in range(0, WIDE, BLOCK):
                 ys = [xs[row(1, t + s + j), :] for j in range(BLOCK)]
                 for n in range(MODES):
                     a = fade[reg(1, n), :]
@@ -409,7 +409,7 @@
                     gate(1, t + at, lambda j, b, at=at: xb[pl.ds((at + j) * SUBS + b, SUBS, stride=SUBS), :])
             return carry
 
-        lax.fori_loop(0, chunk // STEP, body, 0)
+        lax.fori_loop(0, chunk // WIDE, body, 0)
         store(0, c).start()
         store(1, c).start()
     for place in range(2):
@@ -468,7 +468,7 @@
         out_shape=jax.ShapeDtypeStruct((rows, width), jnp.bfloat16),
         in_specs=[vmem] * 5,
         out_specs=hbm,
-        scratch_shapes=[pltpu.VMEM((STEP * SUBS, LANES), F32), registers(MODES), wide, dma((2, PARTS))],
+        scratch_shapes=[pltpu.VMEM((WIDE * SUBS, LANES), F32), registers(MODES), wide, dma((2, PARTS))],
         compiler_params=pltpu.CompilerParams(vmem_limit_bytes=SECOND_VMEM),
     )(*kept)
 

time: 20.2 us -> 20.1 us (level)
  no operation moved by 1% of the time
where the time goes in v9:
time: 20.1 us; the launch traced here: 20 us
  Pallas kernels  20 us (100%)
    pallas_call x1, Pallas kernels, shards(): pl.pallas_call(first_kernel, out_shape=[jax.ShapeDtypeStruct((2 * SPAN *...  16.3 us
    pallas_call x1, Pallas kernels, shards(): pl.pallas_call(second_kernel, out_shape=jax.ShapeDtypeStruct((rows, width...  3.68 us

profile of v9, /device:TPU:34, one launch (start us, length us, event | category | flops | bytes accessed | tf_op | source)
XLA Modules:
  0.0 20.0 jit_solution(4486934622145487174)
XLA Ops:
  0.0 16.3 %shard_map.64 = (f32[8704,128]{1,0:T(8,128)S(1)}, f32[2,16,8,128]{3,2,1,0:T(8,128)S(1)}, f32[256,128]{1,0:T(8,128)S(1)}, f32[256,128]{1,0:T(8,128)S(1)}, bf16[2,512,1024]{2,1,0:T(8,128)(2,1)S(1)}) custom-call(bf16[512,2048]{1,0:T(8,128)(2,1)} %q_hbm.1, bf16[512,2048]{1,0:T(8,128)(2,1)} %k_hbm.1, bf16[512,2048]{1,0:T(8,128)(2,1)} %v_hbm.1, f32[16,2048]{1,0:T(8,128)} %r_hbm.1, ...), custom_call_target="tpu_custom_call" | custom-call | tf_op jit(solution)/shard_map/pallas_call | solution.py:435
  16.3 3.7 %shard_map.65 = bf16[512,2048]{1,0:T(8,128)(2,1)} custom-call(f32[8704,128]{1,0:T(8,128)S(1)} %get-tuple-element.10.xs, f32[2,16,8,128]{3,2,1,0:T(8,128)S(1)} %get-tuple-element.11.enter, f32[256,128]{1,0:T(8,128)S(1)} %get-tuple-element.12.fade, f32[256,128]{1,0:T(8,128)S(1)} %get-tuple-element.13.amp, bf16[2,512,1024]{2,1,0:T(8,128)(2,1)S(1)} %get-tuple-element.14.qb), custom_call_target="tpu_custom_call" | custom-call | tf_op jit(solution)/shard_map/pallas_call | solution.py:466
